TPU v7x, 32 devices: a whole 2x2x4 slice. The times are simulated.
32 devices in a mesh: page: 8 (over z, x), seq: 4 (over y, core).
Axes of the slice: x: 2, y: 2, z: 4, core: 2. Of those that a mesh axis runs over, the one named last changes fastest.
Arguments:
- tokens: bfloat16 [16, 512, 1024], P('page', 'seq'), may hold values from -6 to 6
- cells: int32 [16, 512], P('page', 'seq'), may hold values from 0 to 511, as said below
- lengths: int32 [16], P('page'), may hold values from 64 to 512, as said below
- cotangent: bfloat16 [16, 512, 1024], P('page', 'seq'), may hold values from -6 to 6
- w_qkv: float32 [1024, 3072], P(('page', 'seq')), may hold values from -0.1875 to 0.1875
- w_out: float32 [1024, 1024], P(('page', 'seq')), may hold values from -0.75 to 0.75
- w_up: float32 [1024, 4096], P(('page', 'seq')), may hold values from -0.1875 to 0.1875
- w_down: float32 [4096, 1024], P(('page', 'seq')), may hold values from -0.09375 to 0.09375
- biases: float32 [10, 1024], P(None, ('page', 'seq')), may hold values from -3 to 3
- gains: float32 [2, 1024], P(None, ('page', 'seq')), may hold values from 0.5 to 1.5
- cell_bias: float32 [16], replicated, may hold values from 0.5 to 2
Outputs:
- output: bfloat16 [16, 512, 1024], P('page', 'seq')
- grad_tokens: float32 [16, 512, 1024], P('page', 'seq')
- grad_qkv: float32 [1024, 3072], P(('page', 'seq'))
- grad_out: float32 [1024, 1024], P(('page', 'seq'))
- grad_up: float32 [1024, 4096], P(('page', 'seq'))
- grad_down: float32 [4096, 1024], P(('page', 'seq'))
- grad_biases: float32 [10, 1024], P(None, ('page', 'seq'))
- grad_gains: float32 [2, 1024], P(None, ('page', 'seq'))
- grad_cell: float32 [16], replicated
Inputs may be any that keep to these rules, and one draw needn't show every extreme that they name: `lengths`: every page has at least 64 valid tokens, and some page is full. `cells`: within a page cell numbers never fall, rise by at most one from token to token, and the first token is in cell 0; some page has every token in a cell of its own.
All inputs are finite; a program needn't handle non-finite values.
Results may differ from a plain program's by a relative error of at most 0.014.
The roundings to bfloat16 on the way count: a program that leaves them out, or rounds other values in their place, can miss the bound.
Values may be sent and summed in bfloat16 or wider, within the bound.
No kernel may reach another device: no remote copies, remote signals or barrier semaphores. Data moves between devices by JAX's collectives and lax.ppermute only.
A program may use at most 256 MiB of HBM per device.

v0:
```python
import jax
import jax.numpy as jnp
from jax import lax
from jax.sharding import PartitionSpec as P

LOW = jnp.bfloat16
WIDE = jnp.float32


def layer_norm(values, gain, shift):
    center = values - jnp.mean(values, axis=-1, keepdims=True)
    spread = jnp.mean(center * center, axis=-1, keepdims=True)
    return center * lax.rsqrt(spread + 1e-05) * gain + shift


def gelu_exact(values):
    return 0.5 * values * (1.0 + jax.scipy.special.erf(values * 0.7071067811865476))


def swap(values, axis, count, mask):
    return lax.ppermute(values, axis, [(i, i ^ mask) for i in range(count)])


def bits_of(count):
    return [1 << k for k in range(count.bit_length() - 1)]


def gather_bits(values, axis, count, dim, order):
    index = lax.axis_index(axis)
    done = []
    for mask in order:
        other = swap(values, axis, count, mask)
        place = dim + sum((1 for m in done if m > mask))
        first = index // mask % 2 == 0
        values = jnp.stack(
            [jnp.where(first, values, other), jnp.where(first, other, values)], axis=place
        )
        done.append(mask)
    shape = values.shape
    rest = shape[dim + len(order) :]
    return values.reshape(shape[:dim] + (count,) + rest)


def scatter_bits(values, axis, count, dim, order):
    index = lax.axis_index(axis)
    left = sorted(order, reverse=True)
    shape = values.shape
    values = values.reshape(shape[:dim] + (2,) * len(left) + shape[dim + 1 :])
    for mask in order:
        at = dim + left.index(mask)
        bit = index // mask % 2
        keep = lax.dynamic_index_in_dim(values, bit, at, keepdims=False)
        send = lax.dynamic_index_in_dim(values, 1 - bit, at, keepdims=False)
        values = keep.astype(WIDE) + swap(send.astype(LOW), axis, count, mask).astype(WIDE)
        left.remove(mask)
    return values


def local(
    counts, tokens, cells, lengths, cotangent, w_qkv, w_out, w_up, w_down, biases, gains, cell_bias
):
    pages, seqs = counts
    page_count, row_count, width = tokens.shape
    slots = row_count * seqs
    heads = cell_bias.shape[0]
    depth = width // heads
    heads_here = heads // seqs
    span = heads_here * depth
    flat = page_count * row_count
    rows = w_qkv.shape[0]
    ff_rows = w_down.shape[0]
    ff_here = ff_rows * pages
    seq_index = lax.axis_index("seq")
    high_page = bits_of(pages)[::-1]
    low_page = bits_of(pages)
    high_seq = bits_of(seqs)[::-1]
    low_seq = bits_of(seqs)

    def gather_seq(values, dim):
        return gather_bits(values, "seq", seqs, dim, high_seq)

    def scatter_seq(values, dim):
        return scatter_bits(values, "seq", seqs, dim, low_seq)

    def turn(values):
        return lax.all_to_all(values, "seq", 0, 0)

    part_qkv = w_qkv.astype(LOW).reshape(rows, 3, seqs, span).transpose(2, 0, 1, 3)
    part_qkv = turn(part_qkv.reshape(seqs, rows, 3 * span)).reshape(seqs * rows, 3 * span)
    w_proj = gather_bits(part_qkv, "page", pages, 0, high_page).reshape(width, 3 * span)
    small = jnp.concatenate([biases, gains], axis=0).astype(LOW)
    small_rows = small.shape[0]
    small_pad = -(-small.size // width)
    small_pad = -(-small_pad // 8) * 8
    small_flat = jnp.pad(small.reshape(-1), (0, small_pad * width - small.size)).reshape(
        small_pad, width
    )
    both = lax.all_gather(
        jnp.concatenate([w_out.astype(LOW), small_flat], axis=0),
        ("page", "seq"),
        axis=0,
        tiled=False,
    )
    w_mix = both[:, :rows].reshape(width, width)
    lanes = small.shape[1]
    vectors = both[:, rows:].reshape(pages * seqs, small_pad * width)[:, : small.size]
    vectors = vectors.reshape(pages * seqs, small_rows, lanes).transpose(1, 0, 2)
    vectors = vectors.reshape(small_rows, width).astype(WIDE)
    scales = vectors[small_rows - 2 :]
    part_up = w_up.astype(LOW).reshape(rows, pages, seqs, ff_rows).transpose(2, 0, 1, 3)
    part_up = turn(part_up.reshape(seqs, rows, ff_here)).reshape(seqs * rows, ff_here)
    w_expand = gather_bits(part_up, "page", pages, 0, high_page).reshape(width, ff_here)
    w_reduce = gather_bits(w_down.astype(LOW), "page", pages, 0, high_page).reshape(ff_here, width)
    hidden_bias = vectors[6:10].reshape(pages, seqs, ff_rows)
    hidden_bias = lax.dynamic_index_in_dim(hidden_bias, seq_index, 1, keepdims=False).reshape(
        ff_here
    )
    everything = gather_seq(tokens, 1).reshape(page_count * slots, width)
    cells_all = lax.all_gather(cells, "seq", axis=1, tiled=True)
    bias_q = lax.dynamic_slice_in_dim(vectors[0], seq_index * span, span)
    bias_v = lax.dynamic_slice_in_dim(vectors[1], seq_index * span, span)
    bias_qkv = jnp.concatenate([bias_q, jnp.zeros_like(bias_q), bias_v])
    projected = (jnp.dot(everything, w_proj, preferred_element_type=WIDE) + bias_qkv).astype(LOW)
    projected = projected.reshape(page_count, slots, 3, heads_here, depth)
    query, keys, values = (projected[:, :, 0], projected[:, :, 1], projected[:, :, 2])
    own_bias = lax.dynamic_slice_in_dim(cell_bias, seq_index * heads_here, heads_here)
    same_cell = (cells_all[:, :, None] == cells_all[:, None, :]).astype(WIDE)
    key_valid = lax.broadcasted_iota(jnp.int32, (page_count, slots), 1) < lengths[:, None]

    def scores_of():
        raw = jnp.einsum("pqhe,pkhe->phqk", query, keys, preferred_element_type=WIDE) * 0.125
        scores = raw + own_bias[None, :, None, None] * same_cell[:, None]
        return jnp.where(key_valid[:, None, None, :], scores, -1e30)

    scores = scores_of()
    peak = jnp.max(scores, axis=-1, keepdims=True)
    exponent = jnp.exp(scores - peak)
    totals = jnp.sum(exponent, axis=-1, keepdims=True)
    log_total = peak + jnp.log(totals)
    weights_low = (exponent / totals).astype(LOW)
    context_here = jnp.einsum("phqk,pkhe->pqhe", weights_low, values, preferred_element_type=WIDE)
    context_here = context_here.astype(LOW).reshape(page_count, seqs, row_count, span)
    context = turn(context_here.transpose(1, 0, 2, 3)).transpose(1, 2, 0, 3).reshape(flat, width)
    inputs_wide = tokens.reshape(flat, width).astype(WIDE)
    attended = jnp.dot(context, w_mix, preferred_element_type=WIDE) + vectors[2]
    normed, norm_first = jax.vjp(layer_norm, inputs_wide + attended, scales[0], vectors[4])
    normed_all = gather_seq(normed.astype(LOW), 0).reshape(seqs * flat, width)
    expanded = jnp.dot(normed_all, w_expand, preferred_element_type=WIDE) + hidden_bias
    activated, gelu_back = jax.vjp(gelu_exact, expanded)
    activated_low = activated.astype(LOW)
    reduced = jnp.dot(activated_low, w_reduce, preferred_element_type=WIDE)
    reduced = scatter_seq(reduced.reshape(seqs, flat, width), 0) + vectors[3]
    output_wide, norm_second = jax.vjp(layer_norm, normed + reduced, scales[1], vectors[5])
    output = output_wide.astype(LOW).reshape(page_count, row_count, width)
    grad_second, grad_gain_two, grad_shift_two = norm_second(
        cotangent.reshape(flat, width).astype(WIDE)
    )
    second_all = gather_seq(grad_second.astype(LOW), 0).reshape(seqs * flat, width)
    grad_activated = jnp.einsum("td,fd->tf", second_all, w_reduce, preferred_element_type=WIDE)
    grad_expanded = gelu_back(grad_activated)[0]
    expanded_low = grad_expanded.astype(LOW)
    grad_normed = jnp.einsum("tf,df->td", expanded_low, w_expand, preferred_element_type=WIDE)
    grad_normed = grad_second + scatter_seq(grad_normed.reshape(seqs, flat, width), 0)
    grad_reduce = jnp.einsum("tf,td->fd", activated_low, second_all, preferred_element_type=WIDE)
    grad_reduce = scatter_bits(
        grad_reduce.reshape(pages, ff_rows, width), "page", pages, 0, low_page
    )
    grad_expand = jnp.einsum("td,tf->df", normed_all, expanded_low, preferred_element_type=WIDE)
    grad_expand = scatter_bits(
        grad_expand.reshape(pages, seqs * rows, ff_here), "page", pages, 0, low_page
    )
    grad_expand = turn(grad_expand.astype(LOW).reshape(seqs, rows, ff_here))
    grad_expand = grad_expand.reshape(seqs, rows, pages, ff_rows).transpose(1, 2, 0, 3)
    grad_expand = grad_expand.reshape(rows, seqs * ff_here).astype(WIDE)
    grad_first, grad_gain_one, grad_shift_one = norm_first(grad_normed)
    first_low = grad_first.astype(LOW)
    grad_context = jnp.einsum("td,cd->tc", first_low, w_mix, preferred_element_type=WIDE).astype(
        LOW
    )
    grad_context = grad_context.reshape(page_count, row_count, seqs, span).transpose(2, 0, 1, 3)
    grad_context = (
        turn(grad_context).transpose(1, 0, 2, 3).reshape(page_count, slots, heads_here, depth)
    )
    grad_mix = jnp.einsum("tc,td->cd", context, first_low, preferred_element_type=WIDE)
    grad_mix = scatter_bits(grad_mix.reshape(pages, seqs, rows, width), "seq", seqs, 1, low_seq)
    grad_mix = scatter_bits(grad_mix, "page", pages, 0, low_page)
    weights_wide = jnp.exp(scores_of() - log_total)
    weights_low = weights_wide.astype(LOW)
    grad_weights = jnp.einsum("pqhe,pkhe->phqk", grad_context, values, preferred_element_type=WIDE)
    inner = jnp.sum(weights_wide * grad_weights, axis=-1, keepdims=True)
    grad_scores = weights_wide * (grad_weights - inner)
    grad_cell = jnp.sum(grad_scores * same_cell[:, None], axis=(0, 2, 3))
    scores_low = grad_scores.astype(LOW)
    grad_values = jnp.einsum(
        "phqk,pqhe->pkhe", weights_low, grad_context, preferred_element_type=WIDE
    )
    grad_query = (
        jnp.einsum("phqk,pkhe->pqhe", scores_low, keys, preferred_element_type=WIDE) * 0.125
    )
    grad_keys = (
        jnp.einsum("phqk,pqhe->pkhe", scores_low, query, preferred_element_type=WIDE) * 0.125
    )
    grad_proj_low = jnp.stack([grad_query, grad_keys, grad_values], axis=2).astype(LOW)
    grad_proj_low = grad_proj_low.reshape(page_count * slots, 3 * span)
    grad_proj = jnp.einsum("td,tc->dc", everything, grad_proj_low, preferred_element_type=WIDE)
    grad_proj = scatter_bits(
        grad_proj.reshape(pages, seqs * rows, 3 * span), "page", pages, 0, low_page
    )
    grad_proj = turn(grad_proj.astype(LOW).reshape(seqs, rows, 3 * span))
    grad_proj = (
        grad_proj.reshape(seqs, rows, 3, span).transpose(1, 2, 0, 3).reshape(rows, 3 * width)
    )
    grad_proj = grad_proj.astype(WIDE)
    grad_inputs = jnp.einsum("tc,dc->td", grad_proj_low, w_proj, preferred_element_type=WIDE)
    grad_inputs = scatter_seq(grad_inputs.reshape(page_count, seqs, row_count, width), 1)
    grad_inputs = grad_first.reshape(page_count, row_count, width) + grad_inputs

    def place(vector, size):
        blank = jnp.zeros((width,), WIDE)
        return lax.dynamic_update_slice_in_dim(blank, vector, seq_index * size, 0)

    hidden = jnp.sum(grad_expanded, axis=0).reshape(pages, 1, ff_rows)
    hidden = lax.dynamic_update_slice_in_dim(
        jnp.zeros((pages, seqs, ff_rows), WIDE), hidden, seq_index, 1
    ).reshape(4, width)
    head_rows = jnp.stack(
        [
            place(jnp.sum(grad_query, axis=(0, 1)).reshape(span), span),
            place(jnp.sum(grad_values, axis=(0, 1)).reshape(span), span),
            jnp.sum(grad_first, axis=0),
            jnp.sum(grad_second, axis=0),
            grad_shift_one,
            grad_shift_two,
        ]
    )
    table = jnp.concatenate(
        [
            head_rows,
            hidden,
            grad_gain_one[None],
            grad_gain_two[None],
            place(grad_cell, heads_here)[None],
        ],
        axis=0,
    )
    for mask in low_seq:
        table = table + swap(table, "seq", seqs, mask)
    for mask in low_page:
        table = table + swap(table, "page", pages, mask)
    own = lax.axis_index("page") * seqs + seq_index
    mine = lax.dynamic_slice_in_dim(table, own * lanes, lanes, axis=1)
    return (
        output,
        grad_inputs,
        grad_proj,
        grad_mix,
        grad_expand,
        grad_reduce,
        mine[:10],
        mine[10:12],
        table[12, :heads],
    )


def solution(mesh):
    counts = (mesh.shape["page"], mesh.shape["seq"])
    placed = (
        P("page", "seq", None),
        P("page", "seq"),
        P("page"),
        P("page", "seq", None),
        P(("page", "seq"), None),
        P(("page", "seq"), None),
        P(("page", "seq"), None),
        P(("page", "seq"), None),
        P(None, ("page", "seq")),
        P(None, ("page", "seq")),
        P(),
    )

    def step(*args):
        return local(counts, *args)

    return jax.shard_map(
        step,
        mesh=mesh,
        in_specs=placed,
        out_specs=(
            P("page", "seq", None),
            P("page", "seq", None),
            P(("page", "seq"), None),
            P(("page", "seq"), None),
            P(("page", "seq"), None),
            P(("page", "seq"), None),
            P(None, ("page", "seq")),
            P(None, ("page", "seq")),
            P(),
        ),
        check_vma=False,
    )
```

profile of v0, /device:TPU:0, one launch (start us, length us, event | category | flops | bytes accessed | tf_op | source)
XLA Modules:
  0.0 497.4 jit_solution(14796424124524267543)
XLA Ops:
  12.6 4.2 all-to-all-start
  17.6 3.2 collective-permute-start.10
  20.8 2.0 collective-permute-start
  23.9 12.6 %all_gather.11 = s32[2,512]{1,0:T(2,128)S(1)} all-gather(s32[2,128]{1,0:T(2,128)S(1)} %copy-done.56), channel_id=1, replica_groups=mesh['page'=8,'seq'=4] {'seq'}, dimensions={1}, use_global_device_ids=true | all-gather | bytes 5120 | tf_op jit(solution)/shard_map/all_gather | solution.py:119
  36.5 4.2 all-to-all-start.2
  42.6 13.6 %collective-permute-done.2 = bf16[128,768]{1,0:T(8,128)(2,1)S(1)} collective-permute-done((bf16[128,768]{1,0:T(8,128)(2,1)S(1)}, bf16[128,768]{1,0:T(8,128)(2,1)S(1)}, u32[]{:S(2)}, u32[]{:S(2)}) %collective-permute-start.2) | collective-permute-done | bytes 196640 | tf_op jit(solution)/shard_map/ppermute | solution.py:21
  57.1 3.0 collective-permute-start.7
  61.4 18.7 %collective-permute-done.3 = bf16[2,128,768]{2,1,0:T(8,128)(2,1)} collective-permute-done((bf16[2,128,768]{2,1,0:T(8,128)(2,1)}, bf16[2,128,768]{2,1,0:T(8,128)(2,1)}, u32[]{:S(2)}, u32[]{:S(2)}) %collective-permute-start.3) | collective-permute-done | bytes 393248 | tf_op jit(solution)/shard_map/ppermute | solution.py:21
  87.0 2.0 collective-permute-start.8
  89.0 7.7 %collective-permute-done.4 = bf16[2,2,128,768]{3,2,1,0:T(8,128)(2,1)S(1)} collective-permute-done((bf16[2,2,128,768]{3,2,1,0:T(8,128)(2,1)S(1)}, bf16[2,2,128,768]{3,2,1,0:T(8,128)(2,1)S(1)}, u32[]{:S(2)}, u32[]{:S(2)}) %collective-permute-start.4) | collective-permute-done | bytes 786464 | tf_op jit(solution)/shard_map/ppermute | solution.py:21
  101.9 5.0 add_convert_fusion
  106.9 5.7 %reshape.329 = bf16[2,512,3,4,64]{4,3,2,1,0:T(4,128)(2,1)} reshape(bf16[1024,768]{1,0:T(8,128)(2,1)} %add_convert_fusion) | data formatting | bytes 3145728 | tf_op jit(solution)/shard_map/reshape | solution.py:124
  112.6 4.3 fusion.69
  116.9 2.3 copy.163
  119.1 2.3 copy.164
  123.0 3.5 fusion.72
  127.7 2.1 copy-done
  132.6 4.1 all-to-all-start.1
  141.2 4.5 all-to-all-done.1
  154.6 9.5 %collective-permute-done.5 = bf16[256,1024]{1,0:T(8,128)(2,1)} collective-permute-done((bf16[256,1024]{1,0:T(8,128)(2,1)S(1)}, bf16[256,1024]{1,0:T(8,128)(2,1)}, u32[]{:S(2)}, u32[]{:S(2)}) %collective-permute-start.5) | collective-permute-done | bytes 524320 | tf_op jit(solution)/shard_map/ppermute | solution.py:21
  169.7 17.9 %collective-permute-done.9 = bf16[2,2,128,1024]{3,2,0,1:T(8,128)(2,1)} collective-permute-done((bf16[2,2,128,1024]{3,2,0,1:T(8,128)(2,1)}, bf16[2,2,128,1024]{3,2,0,1:T(8,128)(2,1)}, u32[]{:S(2)}, u32[]{:S(2)}) %collective-permute-start.9) | collective-permute-done | bytes 1048608 | tf_op jit(solution)/shard_map/ppermute | solution.py:21
  193.6 2.1 copy-done.43
  195.8 4.2 multiply_convert_fusion
  200.0 2.3 fusion.76
  202.3 1.9 copy-done.28
  204.5 2.8 collective-permute-done.13
  207.3 2.2 bitcast_add_fusion.5
  212.3 12.4 %collective-permute-done.14 = bf16[256,1024]{1,0:T(8,128)(2,1)} collective-permute-done((bf16[256,1024]{1,0:T(8,128)(2,1)}, bf16[256,1024]{1,0:T(8,128)(2,1)}, u32[]{:S(2)}, u32[]{:S(2)}) %collective-permute-start.14) | collective-permute-done | bytes 524320 | tf_op jit(solution)/shard_map/ppermute | solution.py:21
  230.1 11.5 %collective-permute-done.15 = bf16[256,1024]{1,0:T(8,128)(2,1)S(1)} collective-permute-done((bf16[256,1024]{1,0:T(8,128)(2,1)S(1)}, bf16[256,1024]{1,0:T(8,128)(2,1)S(1)}, u32[]{:S(2)}, u32[]{:S(2)}) %collective-permute-start.15) | collective-permute-done | bytes 524320 | tf_op jit(solution)/shard_map/ppermute | solution.py:21
  243.8 4.0 copy.136
  247.8 4.0 copy.143
  251.7 13.2 %copy.159 = bf16[1024,1024]{1,0:T(8,128)(2,1)} copy(bf16[1024,1024]{0,1:T(8,128)(2,1)} %bitcast.380) | data formatting | bytes 4194304 | tf_op jit(solution)/shard_map/tf,td->fd/dot_general | solution.py:164
  269.2 4.4 fusion.62
  273.7 2.4 fusion.77
  279.2 2.3 fusion.7
  284.7 2.3 fusion.80
  287.0 2.1 copy-done.23
  292.8 2.4 bitcast_add_fusion.4
  297.0 11.9 %collective-permute-done.29 = bf16[2,2,128,1024]{3,2,1,0:T(8,128)(2,1)} collective-permute-done((bf16[2,2,128,1024]{3,2,1,0:T(8,128)(2,1)}, bf16[2,2,128,1024]{3,2,1,0:T(8,128)(2,1)}, u32[]{:S(2)}, u32[]{:S(2)}) %collective-permute-start.29) | collective-permute-done | bytes 1048608 | tf_op jit(solution)/shard_map/ppermute | solution.py:21
  311.7 19.4 %collective-permute-done.32 = bf16[2,2,128,1024]{3,2,1,0:T(8,128)(2,1)} collective-permute-done((bf16[2,2,128,1024]{3,2,1,0:T(8,128)(2,1)}, bf16[2,2,128,1024]{3,2,1,0:T(8,128)(2,1)}, u32[]{:S(2)}, u32[]{:S(2)}) %collective-permute-start.32) | collective-permute-done | bytes 1048608 | tf_op jit(solution)/shard_map/ppermute | solution.py:21
  337.6 2.4 reshape.299
  341.9 4.1 all-to-all-start.3
  347.5 7.2 %collective-permute-start.31 = (bf16[128,1024]{1,0:T(8,128)(2,1)S(1)}, bf16[128,1024]{1,0:T(8,128)(2,1)S(1)}, u32[]{:S(2)}, u32[]{:S(2)}) collective-permute-start(bf16[128,1024]{1,0:T(8,128)(2,1)S(1)} %fusion.52), channel_id=1, source_target_pairs={{0,16},{4,20},{8,24},{12,28},{16,0},{20,4},{24,8},{28,12},{1,17},{... | collective-permute-start | bytes 786440 | tf_op jit(solution)/shard_map/ppermute | solution.py:21
  357.8 2.1 copy-done.1
  361.1 11.2 %collective-permute-done.31 = bf16[128,1024]{1,0:T(8,128)(2,1)S(1)} collective-permute-done((bf16[128,1024]{1,0:T(8,128)(2,1)S(1)}, bf16[128,1024]{1,0:T(8,128)(2,1)S(1)}, u32[]{:S(2)}, u32[]{:S(2)}) %collective-permute-start.31) | collective-permute-done | bytes 262176 | tf_op jit(solution)/shard_map/ppermute | solution.py:21
  373.1 3.6 all-to-all-start.5
  378.3 4.9 fusion.9
  383.2 5.4 %multiply_reduce_fusion.1 = (f32[2,4,512]{2,1,0:T(4,128)S(1)}, f32[2,4,512,512]{2,3,1,0:T(8,128)S(1)}) fusion(f32[2,4,512,512]{2,3,1,0:T(8,128)} %copy-done, f32[2,4,512]{2,1,0:T(4,128)S(1)} %bitcast.403, bf16[2,512,4,64]{1,3,2,0:T(8,128)(2,1)S(1)} %reshape.300, bf16[2,512,1,4,64]{1,4,3,0,2:T(8,128)(2,1)S(1)} %copy-done.38), kind=kOutput, calls=%fused_computation.2 | convolution fusion | flops 274722816 | bytes 17858560 | tf_op jit(solution)/shard_map/pqhe,pkhe->phqk/dot_general | solution.py:189
  388.7 3.3 multiply_reduce_fusion
  397.9 2.8 copy.137
  400.6 3.8 reshape.328
  404.5 3.9 fusion.79
  411.1 3.8 copy.157
  416.6 5.9 %reshape.325 = bf16[2,2,2,128,768]{4,3,2,1,0:T(8,128)(2,1)} reshape(bf16[2,512,3,4,64]{4,3,2,1,0:T(4,128)(2,1)} %copy.157) | data formatting | bytes 3145728 | tf_op jit(solution)/shard_map/convert_element_type | solution.py:203
  423.0 3.2 fusion.78
  426.3 9.7 %collective-permute-done.37 = f32[13,1024]{1,0:T(8,128)S(1)} collective-permute-done((f32[13,1024]{1,0:T(8,128)S(1)}, f32[13,1024]{1,0:T(8,128)S(1)}, u32[]{:S(2)}, u32[]{:S(2)}) %collective-permute-start.37) | collective-permute-done | bytes 53280 | tf_op jit(solution)/shard_map/ppermute | solution.py:21
  436.6 3.8 collective-permute-done.38
  446.3 2.4 bitcast_add_fusion.2
  454.8 5.4 %collective-permute-done.25 = bf16[8,32,1024]{2,1,0:T(8,128)(2,1)S(1)} collective-permute-done((bf16[8,32,1024]{2,1,0:T(8,128)(2,1)S(1)}, bf16[8,32,1024]{2,1,0:T(8,128)(2,1)S(1)}, u32[]{:S(2)}, u32[]{:S(2)}) %collective-permute-start.25) | collective-permute-done | bytes 524320 | tf_op jit(solution)/shard_map/ppermute | solution.py:21
  466.7 2.5 collective-permute-done.23
  469.9 3.4 all-to-all-start.4
  483.2 1.9 collective-permute-start.28
  485.1 2.3 fusion.24
  487.4 2.0 collective-permute-done.28
  (359 shorter events, 140.4 us)
Async XLA Ops:
  7.2 9.7 %copy-start.39 = (f32[128,1024]{1,0:T(8,128)S(1)}, f32[128,1024]{1,0:T(8,128)}, u32[]{:S(2)}) copy-start(f32[128,1024]{1,0:T(8,128)} %param.18) | copy-start | bytes 1572868
  7.2 15.6 %copy-start.55 = (f32[32,4096]{1,0:T(8,128)S(1)}, f32[32,4096]{1,0:T(8,128)}, u32[]{:S(2)}) copy-start(f32[32,4096]{1,0:T(8,128)} %param.17) | copy-start | bytes 1572868
  7.2 92.6 %all-gather.3.cloned.1.call-start = ((), (), s32[]{:S(2)}) async-start(), calls=%async_computation.6 | async-start | bytes 2703360 | tf_op jit(solution)/shard_map/all_gather | solution.py:98
  11.7 12.1 %copy-start.58 = (f32[16]{0:T(128)S(1)}, f32[16]{0:T(128)}, u32[]{:S(2)}) copy-start(f32[16]{0:T(128)} %param.21) | copy-start | bytes 196
  11.7 12.2 %copy-start.56 = (s32[2,128]{1,0:T(2,128)S(1)}, s32[2,128]{1,0:T(2,128)}, u32[]{:S(2)}) copy-start(s32[2,128]{1,0:T(2,128)} %param.12) | copy-start | bytes 3076
  12.6 23.9 %all-to-all-start = ((bf16[4,32,768]{2,1,0:T(8,128)(2,1)}), bf16[4,32,768]{2,1,0:T(8,128)(2,1)S(1)}, u32[]{:S(2)}, u32[]{:S(2)}) async-start(bf16[4,32,768]{2,1,0:T(8,128)(2,1)} %reshape.285), calls=%async_computation | async-start | bytes 393216 | tf_op jit(solution)/shard_map/all_to_all | solution.py:86
  17.6 65.4 %collective-permute-start.10 = (bf16[128,1024]{1,0:T(8,128)(2,1)}, bf16[128,1024]{1,0:T(8,128)(2,1)}, u32[]{:S(2)}, u32[]{:S(2)}) collective-permute-start(bf16[128,1024]{1,0:T(8,128)(2,1)} %convert_element_type.340), channel_id=1, source_target_pairs={{0,16},{4,20},{8,24},{12,28},{16,0},{20,4},{24,8},{28,12},{1,17},{... | collective-permute-start | bytes 786440 | tf_op jit(solution)/shard_map/ppermute | solution.py:21
  20.8 39.3 %collective-permute-start = (bf16[2,128,1024]{2,1,0:T(8,128)(2,1)}, bf16[2,128,1024]{2,1,0:T(8,128)(2,1)}, u32[]{:S(2)}, u32[]{:S(2)}) collective-permute-start(bf16[2,128,1024]{2,1,0:T(8,128)(2,1)} %param.11), channel_id=1, source_target_pairs={{0,2},{1,3},{2,0},{3,1},{4,6},{5,7},{6,4},{7,5},{8,10},{9,11},{10,... | collective-permute-start | bytes 1572872 | tf_op jit(solution)/shard_map/ppermute | solution.py:21
  36.5 20.5 %copy-start.57 = (s32[2]{0:T(128)S(1)}, s32[2]{0:T(128)}, u32[]{:S(2)}) copy-start(s32[2]{0:T(128)} %param.13) | copy-start | bytes 28
  36.5 20.6 %all-to-all-start.2 = ((bf16[4,32,1024]{2,1,0:T(8,128)(2,1)}), bf16[4,32,1024]{2,1,0:T(8,128)(2,1)}, u32[]{:S(2)}, u32[]{:S(2)}) async-start(bf16[4,32,1024]{2,1,0:T(8,128)(2,1)} %reshape.294), calls=%async_computation.2 | async-start | bytes 524288 | tf_op jit(solution)/shard_map/all_to_all | solution.py:86
  40.7 15.5 %collective-permute-start.2 = (bf16[128,768]{1,0:T(8,128)(2,1)S(1)}, bf16[128,768]{1,0:T(8,128)(2,1)S(1)}, u32[]{:S(2)}, u32[]{:S(2)}) collective-permute-start(bf16[128,768]{1,0:T(8,128)(2,1)S(1)} %bitcast.399), channel_id=1, source_target_pairs={{0,16},{4,20},{8,24},{12,28},{16,0},{20,4},{24,8},{28,12},{1,17},{... | collective-permute-start | bytes 589832 | tf_op jit(solution)/shard_map/ppermute | solution.py:21
  42.6 80.4 %copy-start.2 = (f32[2,512,512]{1,2,0:T(8,128)}, f32[2,512,512]{1,2,0:T(8,128)S(1)}, u32[]{:S(2)}) copy-start(f32[2,512,512]{1,2,0:T(8,128)S(1)} %compare_convert_fusion) | copy-start | bytes 6291460
  57.1 23.0 %collective-permute-start.3 = (bf16[2,128,768]{2,1,0:T(8,128)(2,1)}, bf16[2,128,768]{2,1,0:T(8,128)(2,1)}, u32[]{:S(2)}, u32[]{:S(2)}) collective-permute-start(bf16[2,128,768]{2,1,0:T(8,128)(2,1)} %pad_maximum_fusion.15), channel_id=1, source_target_pairs={{0,8},{4,12},{8,0},{12,4},{16,24},{20,28},{24,16},{28,20},{1,9},{5... | collective-permute-start | bytes 1179656 | tf_op jit(solution)/shard_map/ppermute | solution.py:21
  57.1 27.8 %collective-permute-start.7 = (bf16[128,1024]{1,0:T(8,128)(2,1)}, bf16[128,1024]{1,0:T(8,128)(2,1)S(1)}, u32[]{:S(2)}, u32[]{:S(2)}) collective-permute-start(bf16[128,1024]{1,0:T(8,128)(2,1)} %bitcast.36), channel_id=1, source_target_pairs={{0,16},{4,20},{8,24},{12,28},{16,0},{20,4},{24,8},{28,12},{1,17},{... | collective-permute-start | bytes 786440 | tf_op jit(solution)/shard_map/ppermute | solution.py:21
  81.2 15.5 %collective-permute-start.4 = (bf16[2,2,128,768]{3,2,1,0:T(8,128)(2,1)S(1)}, bf16[2,2,128,768]{3,2,1,0:T(8,128)(2,1)S(1)}, u32[]{:S(2)}, u32[]{:S(2)}) collective-permute-start(bf16[2,2,128,768]{3,2,1,0:T(8,128)(2,1)S(1)} %pad_maximum_fusion.12), channel_id=1, source_target_pairs={{0,4},{4,0},{8,12},{12,8},{16,20},{20,16},{24,28},{28,24},{1,5},{5... | collective-permute-start | bytes 2359304 | tf_op jit(solution)/shard_map/ppermute | solution.py:21
  82.9 15.2 %collective-permute-start.1 = (bf16[2,2,128,1024]{3,2,1,0:T(8,128)(2,1)S(1)}, bf16[2,2,128,1024]{3,2,1,0:T(8,128)(2,1)S(1)}, u32[]{:S(2)}, u32[]{:S(2)}) collective-permute-start(bf16[2,2,128,1024]{3,2,1,0:T(8,128)(2,1)S(1)} %pad_maximum_fusion.7), channel_id=1, source_target_pairs={{0,1},{1,0},{2,3},{3,2},{4,5},{5,4},{6,7},{7,6},{8,9},{9,8},{10,11... | collective-permute-start | bytes 3145736 | tf_op jit(solution)/shard_map/ppermute | solution.py:21
  85.0 51.8 %collective-permute-start.11 = (bf16[2,128,1024]{2,1,0:T(8,128)(2,1)}, bf16[2,128,1024]{2,1,0:T(8,128)(2,1)}, u32[]{:S(2)}, u32[]{:S(2)}) collective-permute-start(bf16[2,128,1024]{2,1,0:T(8,128)(2,1)} %pad_maximum_fusion.14), channel_id=1, source_target_pairs={{0,8},{4,12},{8,0},{12,4},{16,24},{20,28},{24,16},{28,20},{1,9},{5... | collective-permute-start | bytes 1572872 | tf_op jit(solution)/shard_map/ppermute | solution.py:21
  87.0 63.9 %collective-permute-start.8 = (bf16[2,128,1024]{2,1,0:T(8,128)(2,1)}, bf16[2,128,1024]{2,1,0:T(8,128)(2,1)}, u32[]{:S(2)}, u32[]{:S(2)}) collective-permute-start(bf16[2,128,1024]{2,1,0:T(8,128)(2,1)} %pad_maximum_fusion.13), channel_id=1, source_target_pairs={{0,8},{4,12},{8,0},{12,4},{16,24},{20,28},{24,16},{28,20},{1,9},{5... | collective-permute-start | bytes 1572872 | tf_op jit(solution)/shard_map/ppermute | solution.py:21
  132.6 13.0 %all-to-all-start.1 = ((bf16[4,2,128,256]{3,2,1,0:T(8,128)(2,1)}), bf16[4,2,128,256]{3,2,1,0:T(8,128)(2,1)}, u32[]{:S(2)}, u32[]{:S(2)}) async-start(bf16[4,2,128,256]{3,2,1,0:T(8,128)(2,1)} %bitcast.27), calls=%async_computation.1 | async-start | bytes 1048576 | tf_op jit(solution)/shard_map/all_to_all | solution.py:86
  139.3 27.3 %collective-permute-start.12 = (bf16[2,2,128,1024]{3,2,0,1:T(8,128)(2,1)}, bf16[2,2,128,1024]{3,2,0,1:T(8,128)(2,1)}, u32[]{:S(2)}, u32[]{:S(2)}) collective-permute-start(bf16[2,2,128,1024]{3,2,0,1:T(8,128)(2,1)} %pad_maximum_fusion.10), channel_id=1, source_target_pairs={{0,4},{4,0},{8,12},{12,8},{16,20},{20,16},{24,28},{28,24},{1,5},{5... | collective-permute-start | bytes 3145736 | tf_op jit(solution)/shard_map/ppermute | solution.py:21
  150.4 13.6 %collective-permute-start.5 = (bf16[256,1024]{1,0:T(8,128)(2,1)S(1)}, bf16[256,1024]{1,0:T(8,128)(2,1)}, u32[]{:S(2)}, u32[]{:S(2)}) collective-permute-start(bf16[256,1024]{1,0:T(8,128)(2,1)S(1)} %fusion.32), channel_id=1, source_target_pairs={{0,2},{1,3},{2,0},{3,1},{4,6},{5,7},{6,4},{7,5},{8,10},{9,11},{10,... | collective-permute-start | bytes 1572872 | tf_op jit(solution)/shard_map/ppermute | solution.py:21
  153.1 34.5 %collective-permute-start.9 = (bf16[2,2,128,1024]{3,2,0,1:T(8,128)(2,1)}, bf16[2,2,128,1024]{3,2,0,1:T(8,128)(2,1)}, u32[]{:S(2)}, u32[]{:S(2)}) collective-permute-start(bf16[2,2,128,1024]{3,2,0,1:T(8,128)(2,1)} %pad_maximum_fusion.9), channel_id=1, source_target_pairs={{0,4},{4,0},{8,12},{12,8},{16,20},{20,16},{24,28},{28,24},{1,5},{5... | collective-permute-start | bytes 3145736 | tf_op jit(solution)/shard_map/ppermute | solution.py:21
  154.6 12.0 %copy-start.12 = (bf16[2,1,128,1024]{3,2,0,1:T(8,128)(2,1)S(1)}, bf16[2,1,128,1024]{3,2,0,1:T(8,128)(2,1)}, u32[]{:S(2)}) copy-start(bf16[2,1,128,1024]{3,2,0,1:T(8,128)(2,1)} %copy-done.11) | copy-start | bytes 1572868
  154.6 12.0 %copy-start.14 = (bf16[2,1,128,1024]{3,2,0,1:T(8,128)(2,1)S(1)}, bf16[2,1,128,1024]{3,2,0,1:T(8,128)(2,1)}, u32[]{:S(2)}) copy-start(bf16[2,1,128,1024]{3,2,0,1:T(8,128)(2,1)} %copy-done.13) | copy-start | bytes 1572868
  166.6 25.3 %collective-permute-start.6 = (bf16[2,256,1024]{2,1,0:T(8,128)(2,1)}, bf16[2,256,1024]{2,1,0:T(8,128)(2,1)}, u32[]{:S(2)}, u32[]{:S(2)}) collective-permute-start(bf16[2,256,1024]{2,1,0:T(8,128)(2,1)} %pad_maximum_fusion.8), channel_id=1, source_target_pairs={{0,1},{1,0},{2,3},{3,2},{4,5},{5,4},{6,7},{7,6},{8,9},{9,8},{10,11... | collective-permute-start | bytes 3145736 | tf_op jit(solution)/shard_map/ppermute | solution.py:21
  204.4 2.9 collective-permute-start.13
  210.4 14.3 %collective-permute-start.14 = (bf16[256,1024]{1,0:T(8,128)(2,1)}, bf16[256,1024]{1,0:T(8,128)(2,1)}, u32[]{:S(2)}, u32[]{:S(2)}) collective-permute-start(bf16[256,1024]{1,0:T(8,128)(2,1)} %fusion.34), channel_id=1, source_target_pairs={{0,2},{1,3},{2,0},{3,1},{4,6},{5,7},{6,4},{7,5},{8,10},{9,11},{10,... | collective-permute-start | bytes 1572872 | tf_op jit(solution)/shard_map/ppermute | solution.py:21
  212.3 14.2 %copy-start.15 = (bf16[2,128,1024]{2,1,0:T(8,128)(2,1)S(1)}, bf16[2,128,1024]{2,1,0:T(8,128)(2,1)}, u32[]{:S(2)}) copy-start(bf16[2,128,1024]{2,1,0:T(8,128)(2,1)} %param.14) | copy-start | bytes 1572868
  228.3 13.2 %collective-permute-start.15 = (bf16[256,1024]{1,0:T(8,128)(2,1)S(1)}, bf16[256,1024]{1,0:T(8,128)(2,1)S(1)}, u32[]{:S(2)}, u32[]{:S(2)}) collective-permute-start(bf16[256,1024]{1,0:T(8,128)(2,1)S(1)} %get-tuple-element.52), channel_id=1, source_target_pairs={{0,2},{1,3},{2,0},{3,1},{4,6},{5,7},{6,4},{7,5},{8,10},{9,11},{10,... | collective-permute-start | bytes 1572872 | tf_op jit(solution)/shard_map/ppermute | solution.py:21
  242.7 22.3 %collective-permute-start.16 = (bf16[2,256,1024]{2,1,0:T(8,128)(2,1)}, bf16[2,256,1024]{2,1,0:T(8,128)(2,1)}, u32[]{:S(2)}, u32[]{:S(2)}) collective-permute-start(bf16[2,256,1024]{2,1,0:T(8,128)(2,1)} %pad_maximum_fusion.11), channel_id=1, source_target_pairs={{0,1},{1,0},{2,3},{3,2},{4,5},{5,4},{6,7},{7,6},{8,9},{9,8},{10,11... | collective-permute-start | bytes 3145736 | tf_op jit(solution)/shard_map/ppermute | solution.py:21
  277.2 15.6 %collective-permute-start.17 = (bf16[2,256,1024]{2,1,0:T(8,128)(2,1)}, bf16[2,256,1024]{2,1,0:T(8,128)(2,1)}, u32[]{:S(2)}, u32[]{:S(2)}) collective-permute-start(bf16[2,256,1024]{2,1,0:T(8,128)(2,1)} %fusion.23), channel_id=1, source_target_pairs={{0,1},{1,0},{2,3},{3,2},{4,5},{5,4},{6,7},{7,6},{8,9},{9,8},{10,11... | collective-permute-start | bytes 3145736 | tf_op jit(solution)/shard_map/ppermute | solution.py:21
  282.7 26.3 %collective-permute-start.29 = (bf16[2,2,128,1024]{3,2,1,0:T(8,128)(2,1)}, bf16[2,2,128,1024]{3,2,1,0:T(8,128)(2,1)}, u32[]{:S(2)}, u32[]{:S(2)}) collective-permute-start(bf16[2,2,128,1024]{3,2,1,0:T(8,128)(2,1)} %fusion.20), channel_id=1, source_target_pairs={{0,4},{4,0},{8,12},{12,8},{16,20},{20,16},{24,28},{28,24},{1,5},{5... | collective-permute-start | bytes 3145736 | tf_op jit(solution)/shard_map/ppermute | solution.py:21
  290.2 40.9 %collective-permute-start.32 = (bf16[2,2,128,1024]{3,2,1,0:T(8,128)(2,1)}, bf16[2,2,128,1024]{3,2,1,0:T(8,128)(2,1)}, u32[]{:S(2)}, u32[]{:S(2)}) collective-permute-start(bf16[2,2,128,1024]{3,2,1,0:T(8,128)(2,1)} %fusion.21), channel_id=1, source_target_pairs={{0,4},{4,0},{8,12},{12,8},{16,20},{20,16},{24,28},{28,24},{1,5},{5... | collective-permute-start | bytes 3145736 | tf_op jit(solution)/shard_map/ppermute | solution.py:21
  292.8 16.2 %copy-start.26 = (f32[2,2,2,128,1024]{4,3,2,1,0:T(8,128)S(1)}, f32[2,2,2,128,1024]{4,3,2,1,0:T(8,128)}, u32[]{:S(2)}) copy-start(f32[2,2,2,128,1024]{4,3,2,1,0:T(8,128)} %copy-done.25) | copy-start | bytes 12582916
  295.3 35.8 %copy-start.24 = (f32[2,2,2,128,1024]{4,3,2,1,0:T(8,128)S(1)}, f32[2,2,2,128,1024]{4,3,2,1,0:T(8,128)}, u32[]{:S(2)}) copy-start(f32[2,2,2,128,1024]{4,3,2,1,0:T(8,128)} %copy-done.23) | copy-start | bytes 12582916
  295.3 38.5 %collective-permute-start.18 = (bf16[256,1024]{1,0:T(8,128)(2,1)S(1)}, bf16[256,1024]{1,0:T(8,128)(2,1)S(1)}, u32[]{:S(2)}, u32[]{:S(2)}) collective-permute-start(bf16[256,1024]{1,0:T(8,128)(2,1)S(1)} %fusion.35), channel_id=1, source_target_pairs={{0,2},{1,3},{2,0},{3,1},{4,6},{5,7},{6,4},{7,5},{8,10},{9,11},{10,... | collective-permute-start | bytes 1572872 | tf_op jit(solution)/shard_map/ppermute | solution.py:21
  310.6 22.1 %copy-start.7 = (f32[2,2,128,1024]{3,2,1,0:T(8,128)}, f32[2,2,128,1024]{3,2,1,0:T(8,128)S(1)}, u32[]{:S(2)}) copy-start(f32[2,2,128,1024]{3,2,1,0:T(8,128)S(1)} %bitcast_add_fusion.1) | copy-start | bytes 6291460
  311.7 34.4 %collective-permute-start.30 = (bf16[2,128,1024]{2,1,0:T(8,128)(2,1)}, bf16[2,128,1024]{2,1,0:T(8,128)(2,1)}, u32[]{:S(2)}, u32[]{:S(2)}) collective-permute-start(bf16[2,128,1024]{2,1,0:T(8,128)(2,1)} %fusion.38), channel_id=1, source_target_pairs={{0,8},{4,12},{8,0},{12,4},{16,24},{20,28},{24,16},{28,20},{1,9},{5... | collective-permute-start | bytes 1572872 | tf_op jit(solution)/shard_map/ppermute | solution.py:21
  333.7 21.0 %collective-permute-start.33 = (bf16[2,128,1024]{2,1,0:T(8,128)(2,1)}, bf16[2,128,1024]{2,1,0:T(8,128)(2,1)}, u32[]{:S(2)}, u32[]{:S(2)}) collective-permute-start(bf16[2,128,1024]{2,1,0:T(8,128)(2,1)} %fusion.39), channel_id=1, source_target_pairs={{0,8},{4,12},{8,0},{12,4},{16,24},{20,28},{24,16},{28,20},{1,9},{5... | collective-permute-start | bytes 1572872 | tf_op jit(solution)/shard_map/ppermute | solution.py:21
  341.9 31.2 %all-to-all-start.3 = ((bf16[4,2,128,256]{3,2,1,0:T(8,128)(2,1)}), bf16[4,2,128,256]{3,2,1,0:T(8,128)(2,1)}, u32[]{:S(2)}, u32[]{:S(2)}) async-start(bf16[4,2,128,256]{3,2,1,0:T(8,128)(2,1)} %bitcast.387), calls=%async_computation.3 | async-start | bytes 1048576 | tf_op jit(solution)/shard_map/all_to_all | solution.py:86
  347.4 9.6 %copy-start.16 = (bf16[1024,256]{1,0:T(8,128)(2,1)S(1)}, bf16[1024,256]{1,0:T(8,128)(2,1)}, u32[]{:S(2)}) copy-start(bf16[1024,256]{1,0:T(8,128)(2,1)} %copy.140) | copy-start | bytes 1572868
  347.5 24.8 %collective-permute-start.31 = (bf16[128,1024]{1,0:T(8,128)(2,1)S(1)}, bf16[128,1024]{1,0:T(8,128)(2,1)S(1)}, u32[]{:S(2)}, u32[]{:S(2)}) collective-permute-start(bf16[128,1024]{1,0:T(8,128)(2,1)S(1)} %fusion.52), channel_id=1, source_target_pairs={{0,16},{4,20},{8,24},{12,28},{16,0},{20,4},{24,8},{28,12},{1,17},{... | collective-permute-start | bytes 786440 | tf_op jit(solution)/shard_map/ppermute | solution.py:21
  356.8 85.2 %collective-permute-start.34 = (bf16[128,1024]{1,0:T(8,128)(2,1)}, bf16[128,1024]{1,0:T(8,128)(2,1)}, u32[]{:S(2)}, u32[]{:S(2)}) collective-permute-start(bf16[128,1024]{1,0:T(8,128)(2,1)} %fusion.53), channel_id=1, source_target_pairs={{0,16},{4,20},{8,24},{12,28},{16,0},{20,4},{24,8},{28,12},{1,17},{... | collective-permute-start | bytes 786440 | tf_op jit(solution)/shard_map/ppermute | solution.py:21
  360.9 85.3 %collective-permute-start.24 = (bf16[8,2,32,1024]{3,2,1,0:T(8,128)(2,1)}, bf16[8,2,32,1024]{3,2,1,0:T(8,128)(2,1)}, u32[]{:S(2)}, u32[]{:S(2)}) collective-permute-start(bf16[8,2,32,1024]{3,2,1,0:T(8,128)(2,1)} %fusion.19), channel_id=1, source_target_pairs={{0,1},{1,0},{2,3},{3,2},{4,5},{5,4},{6,7},{7,6},{8,9},{9,8},{10,11... | collective-permute-start | bytes 3145736 | tf_op jit(solution)/shard_map/ppermute | solution.py:21
  373.1 70.8 %all-to-all-start.5 = ((bf16[4,32,1024]{2,1,0:T(8,128)(2,1)}), bf16[4,32,1024]{2,1,0:T(8,128)(2,1)S(1)}, u32[]{:S(2)}, u32[]{:S(2)}) async-start(bf16[4,32,1024]{2,1,0:T(8,128)(2,1)} %bitcast.123), calls=%async_computation.5 | async-start | bytes 524288 | tf_op jit(solution)/shard_map/all_to_all | solution.py:86
  378.2 10.4 %slice-start = ((s8[8388608]{0:T(1024)(128)(4,1)}), s8[4194304]{0:T(1024)(128)(4,1)S(1)}, s32[]{:S(2)}) async-start(s8[8388608]{0:T(1024)(128)(4,1)} %bitcast.359), calls=%async_computation.7 | async-start | bytes 8388608
  395.9 12.5 %collective-permute-start.35 = (f32[13,1024]{1,0:T(8,128)S(1)}, f32[13,1024]{1,0:T(8,128)S(1)}, u32[]{:S(2)}, u32[]{:S(2)}) collective-permute-start(f32[13,1024]{1,0:T(8,128)S(1)} %concatenate.16), channel_id=1, source_target_pairs={{0,1},{1,0},{2,3},{3,2},{4,5},{5,4},{6,7},{7,6},{8,9},{9,8},{10,11... | collective-permute-start | bytes 159752 | tf_op jit(solution)/shard_map/ppermute | solution.py:21
  408.4 14.1 %collective-permute-start.36 = (f32[13,1024]{1,0:T(8,128)S(1)}, f32[13,1024]{1,0:T(8,128)S(1)}, u32[]{:S(2)}, u32[]{:S(2)}) collective-permute-start(f32[13,1024]{1,0:T(8,128)S(1)} %add.410), channel_id=1, source_target_pairs={{0,2},{1,3},{2,0},{3,1},{4,6},{5,7},{6,4},{7,5},{8,10},{9,11},{10,... | collective-permute-start | bytes 159752 | tf_op jit(solution)/shard_map/ppermute | solution.py:21
  414.8 35.8 %collective-permute-start.21 = (bf16[2,2,128,768]{3,2,1,0:T(8,128)(2,1)}, bf16[2,2,128,768]{3,2,1,0:T(8,128)(2,1)}, u32[]{:S(2)}, u32[]{:S(2)}) collective-permute-start(bf16[2,2,128,768]{3,2,1,0:T(8,128)(2,1)} %fusion.33), channel_id=1, source_target_pairs={{0,4},{4,0},{8,12},{12,8},{16,20},{20,16},{24,28},{28,24},{1,5},{5... | collective-permute-start | bytes 2359304 | tf_op jit(solution)/shard_map/ppermute | solution.py:21
  422.5 13.4 %collective-permute-start.37 = (f32[13,1024]{1,0:T(8,128)S(1)}, f32[13,1024]{1,0:T(8,128)S(1)}, u32[]{:S(2)}, u32[]{:S(2)}) collective-permute-start(f32[13,1024]{1,0:T(8,128)S(1)} %add.411), channel_id=1, source_target_pairs={{0,4},{4,0},{8,12},{12,8},{16,20},{20,16},{24,28},{28,24},{1,5},{5... | collective-permute-start | bytes 159752 | tf_op jit(solution)/shard_map/ppermute | solution.py:21
  426.3 10.0 %copy-start.21 = (f32[2,2,2,128,1024]{4,3,2,1,0:T(8,128)}, f32[2,2,2,128,1024]{4,3,2,1,0:T(8,128)S(1)}, u32[]{:S(2)}) copy-start(f32[2,2,2,128,1024]{4,3,2,1,0:T(8,128)S(1)} %fusion.78) | copy-start | bytes 12582916
  426.3 15.7 %copy-start.18 = (f32[2,128,1024]{2,1,0:T(8,128)S(1)}, f32[2,128,1024]{2,1,0:T(8,128)}, u32[]{:S(2)}) copy-start(f32[2,128,1024]{2,1,0:T(8,128)} %copy-done.17) | copy-start | bytes 3145732
  436.0 4.3 collective-permute-start.38
  436.5 16.7 %collective-permute-start.19 = (bf16[2,2,128,1024]{3,2,1,0:T(8,128)(2,1)S(1)}, bf16[2,2,128,1024]{3,2,1,0:T(8,128)(2,1)}, u32[]{:S(2)}, u32[]{:S(2)}) collective-permute-start(bf16[2,2,128,1024]{3,2,1,0:T(8,128)(2,1)S(1)} %fusion.18), channel_id=1, source_target_pairs={{0,1},{1,0},{2,3},{3,2},{4,5},{5,4},{6,7},{7,6},{8,9},{9,8},{10,11... | collective-permute-start | bytes 3145736 | tf_op jit(solution)/shard_map/ppermute | solution.py:21
  440.3 5.9 %collective-permute-start.39 = (f32[13,1024]{1,0:T(8,128)S(1)}, f32[13,1024]{1,0:T(8,128)S(1)}, u32[]{:S(2)}, u32[]{:S(2)}) collective-permute-start(f32[13,1024]{1,0:T(8,128)S(1)} %add.413), channel_id=1, source_target_pairs={{0,16},{4,20},{8,24},{12,28},{16,0},{20,4},{24,8},{28,12},{1,17},{... | collective-permute-start | bytes 159752 | tf_op jit(solution)/shard_map/ppermute | solution.py:21
  448.8 11.4 %collective-permute-start.25 = (bf16[8,32,1024]{2,1,0:T(8,128)(2,1)S(1)}, bf16[8,32,1024]{2,1,0:T(8,128)(2,1)S(1)}, u32[]{:S(2)}, u32[]{:S(2)}) collective-permute-start(bf16[8,32,1024]{2,1,0:T(8,128)(2,1)S(1)} %fusion.37), channel_id=1, source_target_pairs={{0,2},{1,3},{2,0},{3,1},{4,6},{5,7},{6,4},{7,5},{8,10},{9,11},{10,... | collective-permute-start | bytes 1572872 | tf_op jit(solution)/shard_map/ppermute | solution.py:21
  452.1 8.3 %collective-permute-start.22 = (bf16[2,128,768]{2,1,0:T(8,128)(2,1)S(1)}, bf16[2,128,768]{2,1,0:T(8,128)(2,1)S(1)}, u32[]{:S(2)}, u32[]{:S(2)}) collective-permute-start(bf16[2,128,768]{2,1,0:T(8,128)(2,1)S(1)} %fusion.50), channel_id=1, source_target_pairs={{0,8},{4,12},{8,0},{12,4},{16,24},{20,28},{24,16},{28,20},{1,9},{5... | collective-permute-start | bytes 1179656 | tf_op jit(solution)/shard_map/ppermute | solution.py:21
  460.3 9.6 %copy-start.19 = (f32[8,32,1024]{2,1,0:T(8,128)}, f32[8,32,1024]{2,1,0:T(8,128)S(1)}, u32[]{:S(2)}) copy-start(f32[8,32,1024]{2,1,0:T(8,128)S(1)} %bitcast_add_fusion.9) | copy-start | bytes 3145732
  460.5 8.7 %collective-permute-start.23 = (bf16[128,768]{1,0:T(8,128)(2,1)S(1)}, bf16[128,768]{1,0:T(8,128)(2,1)S(1)}, u32[]{:S(2)}, u32[]{:S(2)}) collective-permute-start(bf16[128,768]{1,0:T(8,128)(2,1)S(1)} %fusion.57), channel_id=1, source_target_pairs={{0,16},{4,20},{8,24},{12,28},{16,0},{20,4},{24,8},{28,12},{1,17},{... | collective-permute-start | bytes 589832 | tf_op jit(solution)/shard_map/ppermute | solution.py:21
  462.7 10.6 %collective-permute-start.26 = (bf16[2,2,32,1024]{3,2,0,1:T(8,128)(2,1)}, bf16[2,2,32,1024]{3,2,0,1:T(8,128)(2,1)}, u32[]{:S(2)}, u32[]{:S(2)}) collective-permute-start(bf16[2,2,32,1024]{3,2,0,1:T(8,128)(2,1)} %fusion.54), channel_id=1, source_target_pairs={{0,4},{4,0},{8,12},{12,8},{16,20},{20,16},{24,28},{28,24},{1,5},{5... | collective-permute-start | bytes 786440 | tf_op jit(solution)/shard_map/ppermute | solution.py:21
  465.3 19.8 %collective-permute-start.20 = (bf16[2,128,1024]{2,1,0:T(8,128)(2,1)}, bf16[2,128,1024]{2,1,0:T(8,128)(2,1)}, u32[]{:S(2)}, u32[]{:S(2)}) collective-permute-start(bf16[2,128,1024]{2,1,0:T(8,128)(2,1)} %fusion.36), channel_id=1, source_target_pairs={{0,2},{1,3},{2,0},{3,1},{4,6},{5,7},{6,4},{7,5},{8,10},{9,11},{10,... | collective-permute-start | bytes 1572872 | tf_op jit(solution)/shard_map/ppermute | solution.py:21
  469.9 8.7 %all-to-all-start.4 = ((bf16[4,32,768]{2,1,0:T(8,128)(2,1)}), bf16[4,32,768]{2,1,0:T(8,128)(2,1)S(1)}, u32[]{:S(2)}, u32[]{:S(2)}) async-start(bf16[4,32,768]{2,1,0:T(8,128)(2,1)} %bitcast.96), calls=%async_computation.4 | async-start | bytes 393216 | tf_op jit(solution)/shard_map/all_to_all | solution.py:86
  476.0 6.2 %collective-permute-start.27 = (bf16[2,32,1024]{2,1,0:T(8,128)(2,1)}, bf16[2,32,1024]{2,1,0:T(8,128)(2,1)}, u32[]{:S(2)}, u32[]{:S(2)}) collective-permute-start(bf16[2,32,1024]{2,1,0:T(8,128)(2,1)} %fusion.58), channel_id=1, source_target_pairs={{0,8},{4,12},{8,0},{12,4},{16,24},{20,28},{24,16},{28,20},{1,9},{5... | collective-permute-start | bytes 393224 | tf_op jit(solution)/shard_map/ppermute | solution.py:21
  483.2 6.2 %collective-permute-start.28 = (bf16[32,1024]{1,0:T(8,128)(2,1)S(1)}, bf16[32,1024]{1,0:T(8,128)(2,1)S(1)}, u32[]{:S(2)}, u32[]{:S(2)}) collective-permute-start(bf16[32,1024]{1,0:T(8,128)(2,1)S(1)} %fusion.59), channel_id=1, source_target_pairs={{0,16},{4,20},{8,24},{12,28},{16,0},{20,4},{24,8},{28,12},{1,17},{... | collective-permute-start | bytes 196616 | tf_op jit(solution)/shard_map/ppermute | solution.py:21
  (45 other events, 161.3 us)
Sparse Core Ops, SparseCore 0:
  11.5 70.7 all-gather.2
where the time goes:
time: 507 us; the launch traced here: 497 us
  waiting for transfers between devices  166 us (33%)
  local copies, waits for them, and re-layouts  109 us (21%)
  starting transfers between devices  73.7 us (15%)
  other arithmetic  66.7 us (13%)
  matrix products  52.9 us (10%)
  between operations  16 us (3%)
  blocking collectives  12.6 us (2%)
    ppermute x40, waiting for transfers between devices, swap(): return lax.ppermute(values, axis, [(i, i ^ mask) for i in range(count)])  161 us
    ppermute x40, starting transfers between devices, swap(): return lax.ppermute(values, axis, [(i, i ^ mask) for i in range(count)])  50 us
    another operation x30, other arithmetic, gather_bits(): jnp.stack([jnp.where(first, values, other), jnp.where(first, other, value...  24.7 us
    unnamed x130, local copies, waits for them, and re-layouts  24.1 us
    all_to_all x6, starting transfers between devices, turn(): return lax.all_to_all(values, 'seq', 0, 0)  23.7 us
    add x15, other arithmetic, scatter_bits(): keep.astype(WIDE) + swap(send.astype(LOW), axis, count, mask).astype(WIDE)  20.7 us
    convert_element_type x3, local copies, waits for them, and re-layouts, local(): jnp.stack([grad_query, grad_keys, grad_values], axis=2).astype(LOW)  13.5 us
    dot_general x1, local copies, waits for them, and re-layouts, local(): jnp.einsum('tf,td->fd', activated_low, second_all, preferred_element_type...  13.2 us
  transfers between devices with their start and end apart: 47, of which 21 were waited for; matrix products, arithmetic and copies ran while one was open for 36% of the time, Pallas kernels for 0%

commit v1 on v0

--- a/solution.py
+++ b/solution.py
@@ -116,7 +116,23 @@
         ff_here
     )
     everything = gather_seq(tokens, 1).reshape(page_count * slots, width)
-    cells_all = lax.all_gather(cells, "seq", axis=1, tiled=True)
+    devices, position, extent = (lax.axis_size("seq"), lax.axis_index("seq"), cells.shape[1])
+    ahead = [(i_2, (i_2 + 1) % devices) for i_2 in range(devices)]
+    backward = [(i_2, (i_2 - 1) % devices) for i_2 in range(devices)]
+    cells_all = jnp.zeros((*cells.shape[:1], devices * extent, *cells.shape[1 + 1 :]), cells.dtype)
+    cells_all = lax.dynamic_update_slice_in_dim(cells_all, cells, position * extent, axis=1)
+    from_left = from_right = cells
+    middle = devices // 2
+    for step_2 in range(1, middle + 1):
+        from_left = lax.ppermute(from_left, "seq", ahead)
+        cells_all = lax.dynamic_update_slice_in_dim(
+            cells_all, from_left, (position - step_2) % devices * extent, axis=1
+        )
+        if step_2 < devices - middle:
+            from_right = lax.ppermute(from_right, "seq", backward)
+            cells_all = lax.dynamic_update_slice_in_dim(
+                cells_all, from_right, (position + step_2) % devices * extent, axis=1
+            )
     bias_q = lax.dynamic_slice_in_dim(vectors[0], seq_index * span, span)
     bias_v = lax.dynamic_slice_in_dim(vectors[1], seq_index * span, span)
     bias_qkv = jnp.concatenate([bias_q, jnp.zeros_like(bias_q), bias_v])

time: 507 us -> 490 us (0.966)
  blocking collectives: 12.6 us -> 0 us
  waiting for transfers between devices: 166 us -> 177 us
  starting transfers between devices: 73.7 us -> 66.5 us
    all_gather x1 -> x0, blocking collectives: 12.6 us -> none  [local(): cells_all = lax.all_gather(cells, 'seq', axis=1, tiled=True)]
    ppermute x40, starting transfers between devices: 50 us -> 42.6 us  [swap(): return lax.ppermute(values, axis, [(i, i ^ mask) for i in range(count)])]
    ppermute x0 -> x3, waiting for transfers between devices: none -> 5.3 us  [the longest x2 5.29 us: local(): from_left = lax.ppermute(from_left, 'seq', ahead)]
    unnamed x130 -> x134, local copies, waits for them, and re-layouts: 24.1 us -> 25.1 us
  transfers between devices with their start and end apart: 47 -> 50, of which waited for: 21 -> 22; matrix products, arithmetic and copies ran while one was open for 36% -> 36% of each run, Pallas kernels for 0% -> 0%
where the time goes in v1:
time: 490 us; the launch traced here: 481 us
  waiting for transfers between devices  177 us (36%)
  local copies, waits for them, and re-layouts  106 us (22%)
  starting transfers between devices  66.5 us (14%)
  other arithmetic  63.1 us (13%)
  matrix products  52.2 us (11%)
  between operations  16.2 us (3%)
    ppermute x40, waiting for transfers between devices, swap(): return lax.ppermute(values, axis, [(i, i ^ mask) for i in range(count)])  165 us
    ppermute x40, starting transfers between devices, swap(): return lax.ppermute(values, axis, [(i, i ^ mask) for i in range(count)])  42.6 us
    unnamed x134, local copies, waits for them, and re-layouts  25.1 us
    all_to_all x6, starting transfers between devices, turn(): return lax.all_to_all(values, 'seq', 0, 0)  21.4 us
    add x15, other arithmetic, scatter_bits(): keep.astype(WIDE) + swap(send.astype(LOW), axis, count, mask).astype(WIDE)  20.7 us
    another operation x30, other arithmetic, gather_bits(): jnp.stack([jnp.where(first, values, other), jnp.where(first, other, value...  20.4 us
    convert_element_type x3, local copies, waits for them, and re-layouts, local(): jnp.stack([grad_query, grad_keys, grad_values], axis=2).astype(LOW)  13.4 us
    dot_general x1, local copies, waits for them, and re-layouts, local(): jnp.einsum('tf,td->fd', activated_low, second_all, preferred_element_type...  13.2 us
  transfers between devices with their start and end apart: 50, of which 22 were waited for; matrix products, arithmetic and copies ran while one was open for 36% of the time, Pallas kernels for 0%

profile of v1, /device:TPU:0, one launch (start us, length us, event | category | flops | bytes accessed | tf_op | source)
XLA Modules:
  0.0 481.2 jit_solution(7653901714829681170)
XLA Ops:
  10.5 2.5 collective-permute-start.6
  15.1 3.4 all-to-all-start
  18.5 2.7 collective-permute-start.13
  21.2 2.0 collective-permute-start
  24.6 3.4 all-to-all-start.2
  28.1 2.3 collective-permute-start.2
  30.3 5.3 %collective-permute-done.7 = s32[2,128]{1,0:T(2,128)S(1)} collective-permute-done((s32[2,128]{1,0:T(2,128)S(1)}, s32[2,128]{1,0:T(2,128)S(1)}, u32[]{:S(2)}, u32[]{:S(2)}) %collective-permute-start.7) | collective-permute-done | bytes 1056 | tf_op jit(solution)/shard_map/ppermute | solution.py:127
  35.6 8.6 %collective-permute-done.2 = bf16[128,768]{1,0:T(8,128)(2,1)S(1)} collective-permute-done((bf16[128,768]{1,0:T(8,128)(2,1)S(1)}, bf16[128,768]{1,0:T(8,128)(2,1)S(1)}, u32[]{:S(2)}, u32[]{:S(2)}) %collective-permute-start.2) | collective-permute-done | bytes 196640 | tf_op jit(solution)/shard_map/ppermute | solution.py:21
  46.6 3.4 collective-permute-start.10
  50.1 14.2 %collective-permute-done.3 = bf16[2,128,768]{2,1,0:T(8,128)(2,1)} collective-permute-done((bf16[2,128,768]{2,1,0:T(8,128)(2,1)S(1)}, bf16[2,128,768]{2,1,0:T(8,128)(2,1)}, u32[]{:S(2)}, u32[]{:S(2)}) %collective-permute-start.3) | collective-permute-done | bytes 393248 | tf_op jit(solution)/shard_map/ppermute | solution.py:21
  70.0 2.0 collective-permute-start.11
  72.0 17.3 %collective-permute-done.4 = bf16[2,2,128,768]{3,2,1,0:T(8,128)(2,1)S(1)} collective-permute-done((bf16[2,2,128,768]{3,2,1,0:T(8,128)(2,1)S(1)}, bf16[2,2,128,768]{3,2,1,0:T(8,128)(2,1)S(1)}, u32[]{:S(2)}, u32[]{:S(2)}) %collective-permute-start.4) | collective-permute-done | bytes 786464 | tf_op jit(solution)/shard_map/ppermute | solution.py:21
  93.7 4.4 add_convert_fusion
  98.1 4.6 reshape.329
  102.7 2.4 fusion.69
  105.1 2.4 copy.163
  107.5 2.3 copy.164
  111.3 3.5 fusion.72
  116.1 2.1 copy-done
  121.0 3.5 all-to-all-start.1
  128.4 4.9 %all-to-all-done.1 = bf16[4,2,128,256]{3,2,1,0:T(8,128)(2,1)S(1)} async-done(((bf16[4,2,128,256]{3,2,1,0:T(8,128)(2,1)}), bf16[4,2,128,256]{3,2,1,0:T(8,128)(2,1)S(1)}, u32[]{:S(2)}, u32[]{:S(2)}) %all-to-all-start.1) | async-done | bytes 524320 | tf_op jit(solution)/shard_map/all_to_all | solution.py:86
  140.6 10.2 %collective-permute-done.8 = bf16[256,1024]{1,0:T(8,128)(2,1)} collective-permute-done((bf16[256,1024]{1,0:T(8,128)(2,1)S(1)}, bf16[256,1024]{1,0:T(8,128)(2,1)}, u32[]{:S(2)}, u32[]{:S(2)}) %collective-permute-start.8) | collective-permute-done | bytes 524320 | tf_op jit(solution)/shard_map/ppermute | solution.py:21
  156.5 18.9 %collective-permute-done.12 = bf16[2,2,128,1024]{3,2,0,1:T(8,128)(2,1)} collective-permute-done((bf16[2,2,128,1024]{3,2,0,1:T(8,128)(2,1)}, bf16[2,2,128,1024]{3,2,0,1:T(8,128)(2,1)}, u32[]{:S(2)}, u32[]{:S(2)}) %collective-permute-start.12) | collective-permute-done | bytes 1048608 | tf_op jit(solution)/shard_map/ppermute | solution.py:21
  181.4 2.1 copy-done.44
  183.6 4.2 multiply_convert_fusion
  187.8 2.3 fusion.76
  192.3 2.8 collective-permute-done.16
  195.1 2.2 bitcast_add_fusion.5
  200.1 12.4 %collective-permute-done.17 = bf16[256,1024]{1,0:T(8,128)(2,1)} collective-permute-done((bf16[256,1024]{1,0:T(8,128)(2,1)}, bf16[256,1024]{1,0:T(8,128)(2,1)}, u32[]{:S(2)}, u32[]{:S(2)}) %collective-permute-start.17) | collective-permute-done | bytes 524320 | tf_op jit(solution)/shard_map/ppermute | solution.py:21
  217.9 11.5 %collective-permute-done.18 = bf16[256,1024]{1,0:T(8,128)(2,1)S(1)} collective-permute-done((bf16[256,1024]{1,0:T(8,128)(2,1)S(1)}, bf16[256,1024]{1,0:T(8,128)(2,1)S(1)}, u32[]{:S(2)}, u32[]{:S(2)}) %collective-permute-start.18) | collective-permute-done | bytes 524320 | tf_op jit(solution)/shard_map/ppermute | solution.py:21
  231.6 3.9 copy.136
  235.6 4.0 copy.143
  239.5 13.2 %copy.159 = bf16[1024,1024]{1,0:T(8,128)(2,1)} copy(bf16[1024,1024]{0,1:T(8,128)(2,1)} %bitcast.380) | data formatting | bytes 4194304 | tf_op jit(solution)/shard_map/tf,td->fd/dot_general | solution.py:180
  257.1 4.4 fusion.62
  261.5 2.4 fusion.77
  267.0 2.3 fusion.7
  272.5 2.3 fusion.80
  274.8 2.1 copy-done.25
  280.0 2.4 bitcast_add_fusion.4
  284.2 12.5 %collective-permute-done.32 = bf16[2,2,128,1024]{3,2,1,0:T(8,128)(2,1)} collective-permute-done((bf16[2,2,128,1024]{3,2,1,0:T(8,128)(2,1)}, bf16[2,2,128,1024]{3,2,1,0:T(8,128)(2,1)}, u32[]{:S(2)}, u32[]{:S(2)}) %collective-permute-start.32) | collective-permute-done | bytes 1048608 | tf_op jit(solution)/shard_map/ppermute | solution.py:21
  299.5 19.4 %collective-permute-done.35 = bf16[2,2,128,1024]{3,2,1,0:T(8,128)(2,1)} collective-permute-done((bf16[2,2,128,1024]{3,2,1,0:T(8,128)(2,1)}, bf16[2,2,128,1024]{3,2,1,0:T(8,128)(2,1)}, u32[]{:S(2)}, u32[]{:S(2)}) %collective-permute-start.35) | collective-permute-done | bytes 1048608 | tf_op jit(solution)/shard_map/ppermute | solution.py:21
  325.4 2.4 reshape.299
  329.7 4.1 all-to-all-start.3
  335.3 3.0 collective-permute-start.34
  341.3 2.1 copy-done.1
  344.7 12.0 %collective-permute-done.34 = bf16[128,1024]{1,0:T(8,128)(2,1)S(1)} collective-permute-done((bf16[128,1024]{1,0:T(8,128)(2,1)S(1)}, bf16[128,1024]{1,0:T(8,128)(2,1)S(1)}, u32[]{:S(2)}, u32[]{:S(2)}) %collective-permute-start.34) | collective-permute-done | bytes 262176 | tf_op jit(solution)/shard_map/ppermute | solution.py:21
  357.4 3.6 all-to-all-start.5
  362.6 4.9 %fusion.9 = f32[2,512,4,64]{1,3,2,0:T(8,128)S(1)} fusion(bf16[2,512,4,64]{1,3,2,0:T(8,128)(2,1)S(1)} %reshape.300, f32[2,4,512,512]{2,3,1,0:T(8,128)} %copy-done, f32[2,4,512]{2,1,0:T(4,128)S(1)} %bitcast.405), kind=kOutput, calls=%fused_computation.43 | convolution fusion | flops 272629760 | bytes 9977856 | tf_op jit(solution)/shard_map/phqk,pqhe->pkhe/dot_general | solution.py:210
  367.6 5.4 %multiply_reduce_fusion.1 = (f32[2,4,512]{2,1,0:T(4,128)S(1)}, f32[2,4,512,512]{2,3,1,0:T(8,128)S(1)}) fusion(f32[2,4,512,512]{2,3,1,0:T(8,128)} %copy-done, f32[2,4,512]{2,1,0:T(4,128)S(1)} %bitcast.406, bf16[2,512,4,64]{1,3,2,0:T(8,128)(2,1)S(1)} %reshape.300, bf16[2,512,1,4,64]{1,4,3,0,2:T(8,128)(2,1)S(1)} %copy-done.40), kind=kOutput, calls=%fused_computation.2 | convolution fusion | flops 274722816 | bytes 17858560 | tf_op jit(solution)/shard_map/pqhe,pkhe->phqk/dot_general | solution.py:205
  373.1 3.3 multiply_reduce_fusion
  382.2 2.8 copy.137
  385.0 3.8 reshape.328
  388.8 3.9 fusion.79
  395.4 3.7 copy.157
  400.6 5.9 %reshape.325 = bf16[2,2,2,128,768]{4,3,2,1,0:T(8,128)(2,1)} reshape(bf16[2,512,3,4,64]{4,3,2,1,0:T(4,128)(2,1)} %copy.157) | data formatting | bytes 3145728 | tf_op jit(solution)/shard_map/convert_element_type | solution.py:219
  407.1 3.2 fusion.78
  410.4 9.8 %collective-permute-done.40 = f32[13,1024]{1,0:T(8,128)S(1)} collective-permute-done((f32[13,1024]{1,0:T(8,128)S(1)}, f32[13,1024]{1,0:T(8,128)S(1)}, u32[]{:S(2)}, u32[]{:S(2)}) %collective-permute-start.40) | collective-permute-done | bytes 53280 | tf_op jit(solution)/shard_map/ppermute | solution.py:21
  420.6 4.0 collective-permute-done.41
  430.0 2.4 bitcast_add_fusion.2
  438.2 5.8 %collective-permute-done.28 = bf16[8,32,1024]{2,1,0:T(8,128)(2,1)S(1)} collective-permute-done((bf16[8,32,1024]{2,1,0:T(8,128)(2,1)S(1)}, bf16[8,32,1024]{2,1,0:T(8,128)(2,1)S(1)}, u32[]{:S(2)}, u32[]{:S(2)}) %collective-permute-start.28) | collective-permute-done | bytes 524320 | tf_op jit(solution)/shard_map/ppermute | solution.py:21
  450.6 2.4 collective-permute-done.26
  453.7 3.4 all-to-all-start.4
  468.9 2.2 fusion.24
  471.1 2.1 collective-permute-done.31
  (373 shorter events, 136.3 us)
Async XLA Ops:
  7.2 16.1 %copy-start.58 = (s32[2,128]{1,0:T(2,128)S(1)}, s32[2,128]{1,0:T(2,128)}, u32[]{:S(2)}) copy-start(s32[2,128]{1,0:T(2,128)} %param.12) | copy-start | bytes 3076
  7.2 14.0 %copy-start.56 = (bf16[2,128,1024]{2,1,0:T(8,128)(2,1)S(1)}, bf16[2,128,1024]{2,1,0:T(8,128)(2,1)}, u32[]{:S(2)}) copy-start(bf16[2,128,1024]{2,1,0:T(8,128)(2,1)} %param.11) | copy-start | bytes 1572868
  7.2 16.0 %copy-start.59 = (s32[2]{0:T(128)S(1)}, s32[2]{0:T(128)}, u32[]{:S(2)}) copy-start(s32[2]{0:T(128)} %param.13) | copy-start | bytes 28
  7.2 16.2 %copy-start.57 = (f32[32,4096]{1,0:T(8,128)S(1)}, f32[32,4096]{1,0:T(8,128)}, u32[]{:S(2)}) copy-start(f32[32,4096]{1,0:T(8,128)} %param.17) | copy-start | bytes 1572868
  7.2 83.9 %all-gather.3.cloned.1.call-start = ((), (), s32[]{:S(2)}) async-start(), calls=%async_computation.6 | async-start | bytes 2703360 | tf_op jit(solution)/shard_map/all_gather | solution.py:98
  10.5 19.9 %collective-permute-start.6 = (s32[2,128]{1,0:T(2,128)}, s32[2,128]{1,0:T(2,128)S(1)}, u32[]{:S(2)}, u32[]{:S(2)}) collective-permute-start(s32[2,128]{1,0:T(2,128)} %param.12), channel_id=1, source_target_pairs={{0,3},{1,0},{2,1},{3,2},{4,7},{5,4},{6,5},{7,6},{8,11},{9,8},{10,9... | collective-permute-start | bytes 3080 | tf_op jit(solution)/shard_map/ppermute | solution.py:132
  12.9 11.7 %collective-permute-start.5 = (s32[2,128]{1,0:T(2,128)}, s32[2,128]{1,0:T(2,128)S(1)}, u32[]{:S(2)}, u32[]{:S(2)}) collective-permute-start(s32[2,128]{1,0:T(2,128)} %param.12), channel_id=1, source_target_pairs={{0,1},{1,2},{2,3},{3,0},{4,5},{5,6},{6,7},{7,4},{8,9},{9,10},{10,1... | collective-permute-start | bytes 3080 | tf_op jit(solution)/shard_map/ppermute | solution.py:127
  15.1 9.5 %all-to-all-start = ((bf16[4,32,768]{2,1,0:T(8,128)(2,1)}), bf16[4,32,768]{2,1,0:T(8,128)(2,1)S(1)}, u32[]{:S(2)}, u32[]{:S(2)}) async-start(bf16[4,32,768]{2,1,0:T(8,128)(2,1)} %reshape.285), calls=%async_computation | async-start | bytes 393216 | tf_op jit(solution)/shard_map/all_to_all | solution.py:86
  18.5 48.6 %collective-permute-start.13 = (bf16[128,1024]{1,0:T(8,128)(2,1)S(1)}, bf16[128,1024]{1,0:T(8,128)(2,1)}, u32[]{:S(2)}, u32[]{:S(2)}) collective-permute-start(bf16[128,1024]{1,0:T(8,128)(2,1)S(1)} %convert_element_type.340), channel_id=1, source_target_pairs={{0,16},{4,20},{8,24},{12,28},{16,0},{20,4},{24,8},{28,12},{1,17},{... | collective-permute-start | bytes 786440 | tf_op jit(solution)/shard_map/ppermute | solution.py:21
  21.2 28.8 %collective-permute-start = (bf16[2,128,1024]{2,1,0:T(8,128)(2,1)S(1)}, bf16[2,128,1024]{2,1,0:T(8,128)(2,1)S(1)}, u32[]{:S(2)}, u32[]{:S(2)}) collective-permute-start(bf16[2,128,1024]{2,1,0:T(8,128)(2,1)S(1)} %copy-done.56), channel_id=1, source_target_pairs={{0,2},{1,3},{2,0},{3,1},{4,6},{5,7},{6,4},{7,5},{8,10},{9,11},{10,... | collective-permute-start | bytes 1572872 | tf_op jit(solution)/shard_map/ppermute | solution.py:21
  24.6 11.0 %collective-permute-start.7 = (s32[2,128]{1,0:T(2,128)S(1)}, s32[2,128]{1,0:T(2,128)S(1)}, u32[]{:S(2)}, u32[]{:S(2)}) collective-permute-start(s32[2,128]{1,0:T(2,128)S(1)} %collective-permute-done.5), channel_id=1, source_target_pairs={{0,1},{1,2},{2,3},{3,0},{4,5},{5,6},{6,7},{7,4},{8,9},{9,10},{10,1... | collective-permute-start | bytes 3080 | tf_op jit(solution)/shard_map/ppermute | solution.py:127
  24.6 22.0 %all-to-all-start.2 = ((bf16[4,32,1024]{2,1,0:T(8,128)(2,1)}), bf16[4,32,1024]{2,1,0:T(8,128)(2,1)S(1)}, u32[]{:S(2)}, u32[]{:S(2)}) async-start(bf16[4,32,1024]{2,1,0:T(8,128)(2,1)} %reshape.294), calls=%async_computation.2 | async-start | bytes 524288 | tf_op jit(solution)/shard_map/all_to_all | solution.py:86
  28.1 16.1 %collective-permute-start.2 = (bf16[128,768]{1,0:T(8,128)(2,1)S(1)}, bf16[128,768]{1,0:T(8,128)(2,1)S(1)}, u32[]{:S(2)}, u32[]{:S(2)}) collective-permute-start(bf16[128,768]{1,0:T(8,128)(2,1)S(1)} %bitcast.401), channel_id=1, source_target_pairs={{0,16},{4,20},{8,24},{12,28},{16,0},{20,4},{24,8},{28,12},{1,17},{... | collective-permute-start | bytes 589832 | tf_op jit(solution)/shard_map/ppermute | solution.py:21
  44.3 20.0 %collective-permute-start.3 = (bf16[2,128,768]{2,1,0:T(8,128)(2,1)S(1)}, bf16[2,128,768]{2,1,0:T(8,128)(2,1)}, u32[]{:S(2)}, u32[]{:S(2)}) collective-permute-start(bf16[2,128,768]{2,1,0:T(8,128)(2,1)S(1)} %pad_maximum_fusion.15), channel_id=1, source_target_pairs={{0,8},{4,12},{8,0},{12,4},{16,24},{20,28},{24,16},{28,20},{1,9},{5... | collective-permute-start | bytes 1179656 | tf_op jit(solution)/shard_map/ppermute | solution.py:21
  46.6 22.4 %collective-permute-start.10 = (bf16[128,1024]{1,0:T(8,128)(2,1)S(1)}, bf16[128,1024]{1,0:T(8,128)(2,1)S(1)}, u32[]{:S(2)}, u32[]{:S(2)}) collective-permute-start(bf16[128,1024]{1,0:T(8,128)(2,1)S(1)} %bitcast.398), channel_id=1, source_target_pairs={{0,16},{4,20},{8,24},{12,28},{16,0},{20,4},{24,8},{28,12},{1,17},{... | collective-permute-start | bytes 786440 | tf_op jit(solution)/shard_map/ppermute | solution.py:21
  65.4 23.9 %collective-permute-start.4 = (bf16[2,2,128,768]{3,2,1,0:T(8,128)(2,1)S(1)}, bf16[2,2,128,768]{3,2,1,0:T(8,128)(2,1)S(1)}, u32[]{:S(2)}, u32[]{:S(2)}) collective-permute-start(bf16[2,2,128,768]{3,2,1,0:T(8,128)(2,1)S(1)} %pad_maximum_fusion.12), channel_id=1, source_target_pairs={{0,4},{4,0},{8,12},{12,8},{16,20},{20,16},{24,28},{28,24},{1,5},{5... | collective-permute-start | bytes 2359304 | tf_op jit(solution)/shard_map/ppermute | solution.py:21
  67.0 23.7 %collective-permute-start.1 = (bf16[2,2,128,1024]{3,2,1,0:T(8,128)(2,1)S(1)}, bf16[2,2,128,1024]{3,2,1,0:T(8,128)(2,1)S(1)}, u32[]{:S(2)}, u32[]{:S(2)}) collective-permute-start(bf16[2,2,128,1024]{3,2,1,0:T(8,128)(2,1)S(1)} %pad_maximum_fusion.7), channel_id=1, source_target_pairs={{0,1},{1,0},{2,3},{3,2},{4,5},{5,4},{6,7},{7,6},{8,9},{9,8},{10,11... | collective-permute-start | bytes 3145736 | tf_op jit(solution)/shard_map/ppermute | solution.py:21
  68.1 21.3 %copy-start.31 = (bf16[1,128,1024]{2,1,0:T(8,128)(2,1)}, bf16[1,128,1024]{2,1,0:T(8,128)(2,1)S(1)}, u32[]{:S(2)}) copy-start(bf16[1,128,1024]{2,1,0:T(8,128)(2,1)S(1)} %get-tuple-element.70) | copy-start | bytes 786436
  69.0 55.5 %collective-permute-start.14 = (bf16[2,128,1024]{2,1,0:T(8,128)(2,1)}, bf16[2,128,1024]{2,1,0:T(8,128)(2,1)}, u32[]{:S(2)}, u32[]{:S(2)}) collective-permute-start(bf16[2,128,1024]{2,1,0:T(8,128)(2,1)} %pad_maximum_fusion.14), channel_id=1, source_target_pairs={{0,8},{4,12},{8,0},{12,4},{16,24},{20,28},{24,16},{28,20},{1,9},{5... | collective-permute-start | bytes 1572872 | tf_op jit(solution)/shard_map/ppermute | solution.py:21
  69.1 20.4 %copy-start.33 = (bf16[1,128,1024]{2,1,0:T(8,128)(2,1)}, bf16[1,128,1024]{2,1,0:T(8,128)(2,1)S(1)}, u32[]{:S(2)}) copy-start(bf16[1,128,1024]{2,1,0:T(8,128)(2,1)S(1)} %get-tuple-element.71) | copy-start | bytes 786436
  69.1 20.4 %copy-start.35 = (bf16[1,128,1024]{2,1,0:T(8,128)(2,1)}, bf16[1,128,1024]{2,1,0:T(8,128)(2,1)S(1)}, u32[]{:S(2)}) copy-start(bf16[1,128,1024]{2,1,0:T(8,128)(2,1)S(1)} %get-tuple-element.72) | copy-start | bytes 786436
  70.0 67.4 %collective-permute-start.11 = (bf16[2,128,1024]{2,1,0:T(8,128)(2,1)}, bf16[2,128,1024]{2,1,0:T(8,128)(2,1)}, u32[]{:S(2)}, u32[]{:S(2)}) collective-permute-start(bf16[2,128,1024]{2,1,0:T(8,128)(2,1)} %pad_maximum_fusion.13), channel_id=1, source_target_pairs={{0,8},{4,12},{8,0},{12,4},{16,24},{20,28},{24,16},{28,20},{1,9},{5... | collective-permute-start | bytes 1572872 | tf_op jit(solution)/shard_map/ppermute | solution.py:21
  121.0 12.3 %all-to-all-start.1 = ((bf16[4,2,128,256]{3,2,1,0:T(8,128)(2,1)}), bf16[4,2,128,256]{3,2,1,0:T(8,128)(2,1)S(1)}, u32[]{:S(2)}, u32[]{:S(2)}) async-start(bf16[4,2,128,256]{3,2,1,0:T(8,128)(2,1)} %bitcast.27), calls=%async_computation.1 | async-start | bytes 1048576 | tf_op jit(solution)/shard_map/all_to_all | solution.py:86
  127.1 26.3 %collective-permute-start.15 = (bf16[2,2,128,1024]{3,2,0,1:T(8,128)(2,1)}, bf16[2,2,128,1024]{3,2,0,1:T(8,128)(2,1)}, u32[]{:S(2)}, u32[]{:S(2)}) collective-permute-start(bf16[2,2,128,1024]{3,2,0,1:T(8,128)(2,1)} %pad_maximum_fusion.10), channel_id=1, source_target_pairs={{0,4},{4,0},{8,12},{12,8},{16,20},{20,16},{24,28},{28,24},{1,5},{5... | collective-permute-start | bytes 3145736 | tf_op jit(solution)/shard_map/ppermute | solution.py:21
  137.0 13.7 %collective-permute-start.8 = (bf16[256,1024]{1,0:T(8,128)(2,1)S(1)}, bf16[256,1024]{1,0:T(8,128)(2,1)}, u32[]{:S(2)}, u32[]{:S(2)}) collective-permute-start(bf16[256,1024]{1,0:T(8,128)(2,1)S(1)} %fusion.32), channel_id=1, source_target_pairs={{0,2},{1,3},{2,0},{3,1},{4,6},{5,7},{6,4},{7,5},{8,10},{9,11},{10,... | collective-permute-start | bytes 1572872 | tf_op jit(solution)/shard_map/ppermute | solution.py:21
  139.7 35.7 %collective-permute-start.12 = (bf16[2,2,128,1024]{3,2,0,1:T(8,128)(2,1)}, bf16[2,2,128,1024]{3,2,0,1:T(8,128)(2,1)}, u32[]{:S(2)}, u32[]{:S(2)}) collective-permute-start(bf16[2,2,128,1024]{3,2,0,1:T(8,128)(2,1)} %pad_maximum_fusion.9), channel_id=1, source_target_pairs={{0,4},{4,0},{8,12},{12,8},{16,20},{20,16},{24,28},{28,24},{1,5},{5... | collective-permute-start | bytes 3145736 | tf_op jit(solution)/shard_map/ppermute | solution.py:21
  140.6 12.8 %copy-start.13 = (bf16[2,1,128,1024]{3,2,0,1:T(8,128)(2,1)S(1)}, bf16[2,1,128,1024]{3,2,0,1:T(8,128)(2,1)}, u32[]{:S(2)}) copy-start(bf16[2,1,128,1024]{3,2,0,1:T(8,128)(2,1)} %copy-done.12) | copy-start | bytes 1572868
  140.6 12.8 %copy-start.15 = (bf16[2,1,128,1024]{3,2,0,1:T(8,128)(2,1)S(1)}, bf16[2,1,128,1024]{3,2,0,1:T(8,128)(2,1)}, u32[]{:S(2)}) copy-start(bf16[2,1,128,1024]{3,2,0,1:T(8,128)(2,1)} %copy-done.14) | copy-start | bytes 1572868
  153.2 26.4 %collective-permute-start.9 = (bf16[2,256,1024]{2,1,0:T(8,128)(2,1)}, bf16[2,256,1024]{2,1,0:T(8,128)(2,1)}, u32[]{:S(2)}, u32[]{:S(2)}) collective-permute-start(bf16[2,256,1024]{2,1,0:T(8,128)(2,1)} %pad_maximum_fusion.8), channel_id=1, source_target_pairs={{0,1},{1,0},{2,3},{3,2},{4,5},{5,4},{6,7},{7,6},{8,9},{9,8},{10,11... | collective-permute-start | bytes 3145736 | tf_op jit(solution)/shard_map/ppermute | solution.py:21
  192.3 2.9 collective-permute-start.16
  198.2 14.3 %collective-permute-start.17 = (bf16[256,1024]{1,0:T(8,128)(2,1)}, bf16[256,1024]{1,0:T(8,128)(2,1)}, u32[]{:S(2)}, u32[]{:S(2)}) collective-permute-start(bf16[256,1024]{1,0:T(8,128)(2,1)} %fusion.34), channel_id=1, source_target_pairs={{0,2},{1,3},{2,0},{3,1},{4,6},{5,7},{6,4},{7,5},{8,10},{9,11},{10,... | collective-permute-start | bytes 1572872 | tf_op jit(solution)/shard_map/ppermute | solution.py:21
  200.1 14.2 %copy-start.16 = (bf16[2,128,1024]{2,1,0:T(8,128)(2,1)S(1)}, bf16[2,128,1024]{2,1,0:T(8,128)(2,1)}, u32[]{:S(2)}) copy-start(bf16[2,128,1024]{2,1,0:T(8,128)(2,1)} %param.14) | copy-start | bytes 1572868
  216.2 13.2 %collective-permute-start.18 = (bf16[256,1024]{1,0:T(8,128)(2,1)S(1)}, bf16[256,1024]{1,0:T(8,128)(2,1)S(1)}, u32[]{:S(2)}, u32[]{:S(2)}) collective-permute-start(bf16[256,1024]{1,0:T(8,128)(2,1)S(1)} %get-tuple-element.52), channel_id=1, source_target_pairs={{0,2},{1,3},{2,0},{3,1},{4,6},{5,7},{6,4},{7,5},{8,10},{9,11},{10,... | collective-permute-start | bytes 1572872 | tf_op jit(solution)/shard_map/ppermute | solution.py:21
  230.5 22.3 %collective-permute-start.19 = (bf16[2,256,1024]{2,1,0:T(8,128)(2,1)}, bf16[2,256,1024]{2,1,0:T(8,128)(2,1)}, u32[]{:S(2)}, u32[]{:S(2)}) collective-permute-start(bf16[2,256,1024]{2,1,0:T(8,128)(2,1)} %pad_maximum_fusion.11), channel_id=1, source_target_pairs={{0,1},{1,0},{2,3},{3,2},{4,5},{5,4},{6,7},{7,6},{8,9},{9,8},{10,11... | collective-permute-start | bytes 3145736 | tf_op jit(solution)/shard_map/ppermute | solution.py:21
  265.0 15.0 %collective-permute-start.20 = (bf16[2,256,1024]{2,1,0:T(8,128)(2,1)}, bf16[2,256,1024]{2,1,0:T(8,128)(2,1)}, u32[]{:S(2)}, u32[]{:S(2)}) collective-permute-start(bf16[2,256,1024]{2,1,0:T(8,128)(2,1)} %fusion.23), channel_id=1, source_target_pairs={{0,1},{1,0},{2,3},{3,2},{4,5},{5,4},{6,7},{7,6},{8,9},{9,8},{10,11... | collective-permute-start | bytes 3145736 | tf_op jit(solution)/shard_map/ppermute | solution.py:21
  270.5 26.3 %collective-permute-start.32 = (bf16[2,2,128,1024]{3,2,1,0:T(8,128)(2,1)}, bf16[2,2,128,1024]{3,2,1,0:T(8,128)(2,1)}, u32[]{:S(2)}, u32[]{:S(2)}) collective-permute-start(bf16[2,2,128,1024]{3,2,1,0:T(8,128)(2,1)} %fusion.20), channel_id=1, source_target_pairs={{0,4},{4,0},{8,12},{12,8},{16,20},{20,16},{24,28},{28,24},{1,5},{5... | collective-permute-start | bytes 3145736 | tf_op jit(solution)/shard_map/ppermute | solution.py:21
  278.0 40.9 %collective-permute-start.35 = (bf16[2,2,128,1024]{3,2,1,0:T(8,128)(2,1)}, bf16[2,2,128,1024]{3,2,1,0:T(8,128)(2,1)}, u32[]{:S(2)}, u32[]{:S(2)}) collective-permute-start(bf16[2,2,128,1024]{3,2,1,0:T(8,128)(2,1)} %fusion.21), channel_id=1, source_target_pairs={{0,4},{4,0},{8,12},{12,8},{16,20},{20,16},{24,28},{28,24},{1,5},{5... | collective-permute-start | bytes 3145736 | tf_op jit(solution)/shard_map/ppermute | solution.py:21
  280.0 16.8 %copy-start.28 = (f32[2,2,2,128,1024]{4,3,2,1,0:T(8,128)S(1)}, f32[2,2,2,128,1024]{4,3,2,1,0:T(8,128)}, u32[]{:S(2)}) copy-start(f32[2,2,2,128,1024]{4,3,2,1,0:T(8,128)} %copy-done.27) | copy-start | bytes 12582916
  282.5 36.4 %copy-start.26 = (f32[2,2,2,128,1024]{4,3,2,1,0:T(8,128)S(1)}, f32[2,2,2,128,1024]{4,3,2,1,0:T(8,128)}, u32[]{:S(2)}) copy-start(f32[2,2,2,128,1024]{4,3,2,1,0:T(8,128)} %copy-done.25) | copy-start | bytes 12582916
  282.5 39.0 %collective-permute-start.21 = (bf16[256,1024]{1,0:T(8,128)(2,1)S(1)}, bf16[256,1024]{1,0:T(8,128)(2,1)S(1)}, u32[]{:S(2)}, u32[]{:S(2)}) collective-permute-start(bf16[256,1024]{1,0:T(8,128)(2,1)S(1)} %fusion.35), channel_id=1, source_target_pairs={{0,2},{1,3},{2,0},{3,1},{4,6},{5,7},{6,4},{7,5},{8,10},{9,11},{10,... | collective-permute-start | bytes 1572872 | tf_op jit(solution)/shard_map/ppermute | solution.py:21
  298.5 22.1 %copy-start.8 = (f32[2,2,128,1024]{3,2,1,0:T(8,128)}, f32[2,2,128,1024]{3,2,1,0:T(8,128)S(1)}, u32[]{:S(2)}) copy-start(f32[2,2,128,1024]{3,2,1,0:T(8,128)S(1)} %bitcast_add_fusion.1) | copy-start | bytes 6291460
  299.5 34.4 %collective-permute-start.33 = (bf16[2,128,1024]{2,1,0:T(8,128)(2,1)}, bf16[2,128,1024]{2,1,0:T(8,128)(2,1)}, u32[]{:S(2)}, u32[]{:S(2)}) collective-permute-start(bf16[2,128,1024]{2,1,0:T(8,128)(2,1)} %fusion.38), channel_id=1, source_target_pairs={{0,8},{4,12},{8,0},{12,4},{16,24},{20,28},{24,16},{28,20},{1,9},{5... | collective-permute-start | bytes 1572872 | tf_op jit(solution)/shard_map/ppermute | solution.py:21
  321.5 16.8 %collective-permute-start.36 = (bf16[2,128,1024]{2,1,0:T(8,128)(2,1)}, bf16[2,128,1024]{2,1,0:T(8,128)(2,1)}, u32[]{:S(2)}, u32[]{:S(2)}) collective-permute-start(bf16[2,128,1024]{2,1,0:T(8,128)(2,1)} %fusion.39), channel_id=1, source_target_pairs={{0,8},{4,12},{8,0},{12,4},{16,24},{20,28},{24,16},{28,20},{1,9},{5... | collective-permute-start | bytes 1572872 | tf_op jit(solution)/shard_map/ppermute | solution.py:21
  329.7 27.7 %all-to-all-start.3 = ((bf16[4,2,128,256]{3,2,1,0:T(8,128)(2,1)}), bf16[4,2,128,256]{3,2,1,0:T(8,128)(2,1)}, u32[]{:S(2)}, u32[]{:S(2)}) async-start(bf16[4,2,128,256]{3,2,1,0:T(8,128)(2,1)} %bitcast.387), calls=%async_computation.3 | async-start | bytes 1048576 | tf_op jit(solution)/shard_map/all_to_all | solution.py:86
  335.3 21.4 %collective-permute-start.34 = (bf16[128,1024]{1,0:T(8,128)(2,1)S(1)}, bf16[128,1024]{1,0:T(8,128)(2,1)S(1)}, u32[]{:S(2)}, u32[]{:S(2)}) collective-permute-start(bf16[128,1024]{1,0:T(8,128)(2,1)S(1)} %fusion.52), channel_id=1, source_target_pairs={{0,16},{4,20},{8,24},{12,28},{16,0},{20,4},{24,8},{28,12},{1,17},{... | collective-permute-start | bytes 786440 | tf_op jit(solution)/shard_map/ppermute | solution.py:21
  340.3 85.2 %collective-permute-start.37 = (bf16[128,1024]{1,0:T(8,128)(2,1)}, bf16[128,1024]{1,0:T(8,128)(2,1)}, u32[]{:S(2)}, u32[]{:S(2)}) collective-permute-start(bf16[128,1024]{1,0:T(8,128)(2,1)} %fusion.53), channel_id=1, source_target_pairs={{0,16},{4,20},{8,24},{12,28},{16,0},{20,4},{24,8},{28,12},{1,17},{... | collective-permute-start | bytes 786440 | tf_op jit(solution)/shard_map/ppermute | solution.py:21
  344.5 85.5 %collective-permute-start.27 = (bf16[8,2,32,1024]{3,2,1,0:T(8,128)(2,1)}, bf16[8,2,32,1024]{3,2,1,0:T(8,128)(2,1)}, u32[]{:S(2)}, u32[]{:S(2)}) collective-permute-start(bf16[8,2,32,1024]{3,2,1,0:T(8,128)(2,1)} %fusion.19), channel_id=1, source_target_pairs={{0,1},{1,0},{2,3},{3,2},{4,5},{5,4},{6,7},{7,6},{8,9},{9,8},{10,11... | collective-permute-start | bytes 3145736 | tf_op jit(solution)/shard_map/ppermute | solution.py:21
  357.4 69.9 %all-to-all-start.5 = ((bf16[4,32,1024]{2,1,0:T(8,128)(2,1)}), bf16[4,32,1024]{2,1,0:T(8,128)(2,1)S(1)}, u32[]{:S(2)}, u32[]{:S(2)}) async-start(bf16[4,32,1024]{2,1,0:T(8,128)(2,1)} %bitcast.123), calls=%async_computation.5 | async-start | bytes 524288 | tf_op jit(solution)/shard_map/all_to_all | solution.py:86
  380.2 12.5 %collective-permute-start.38 = (f32[13,1024]{1,0:T(8,128)S(1)}, f32[13,1024]{1,0:T(8,128)S(1)}, u32[]{:S(2)}, u32[]{:S(2)}) collective-permute-start(f32[13,1024]{1,0:T(8,128)S(1)} %concatenate.16), channel_id=1, source_target_pairs={{0,1},{1,0},{2,3},{3,2},{4,5},{5,4},{6,7},{7,6},{8,9},{9,8},{10,11... | collective-permute-start | bytes 159752 | tf_op jit(solution)/shard_map/ppermute | solution.py:21
  392.7 13.8 %collective-permute-start.39 = (f32[13,1024]{1,0:T(8,128)S(1)}, f32[13,1024]{1,0:T(8,128)S(1)}, u32[]{:S(2)}, u32[]{:S(2)}) collective-permute-start(f32[13,1024]{1,0:T(8,128)S(1)} %add.444), channel_id=1, source_target_pairs={{0,2},{1,3},{2,0},{3,1},{4,6},{5,7},{6,4},{7,5},{8,10},{9,11},{10,... | collective-permute-start | bytes 159752 | tf_op jit(solution)/shard_map/ppermute | solution.py:21
  399.1 35.3 %collective-permute-start.24 = (bf16[2,2,128,768]{3,2,1,0:T(8,128)(2,1)}, bf16[2,2,128,768]{3,2,1,0:T(8,128)(2,1)}, u32[]{:S(2)}, u32[]{:S(2)}) collective-permute-start(bf16[2,2,128,768]{3,2,1,0:T(8,128)(2,1)} %fusion.33), channel_id=1, source_target_pairs={{0,4},{4,0},{8,12},{12,8},{16,20},{20,16},{24,28},{28,24},{1,5},{5... | collective-permute-start | bytes 2359304 | tf_op jit(solution)/shard_map/ppermute | solution.py:21
  406.6 13.7 %collective-permute-start.40 = (f32[13,1024]{1,0:T(8,128)S(1)}, f32[13,1024]{1,0:T(8,128)S(1)}, u32[]{:S(2)}, u32[]{:S(2)}) collective-permute-start(f32[13,1024]{1,0:T(8,128)S(1)} %add.445), channel_id=1, source_target_pairs={{0,4},{4,0},{8,12},{12,8},{16,20},{20,16},{24,28},{28,24},{1,5},{5... | collective-permute-start | bytes 159752 | tf_op jit(solution)/shard_map/ppermute | solution.py:21
  410.4 15.1 %copy-start.20 = (f32[2,128,1024]{2,1,0:T(8,128)S(1)}, f32[2,128,1024]{2,1,0:T(8,128)}, u32[]{:S(2)}) copy-start(f32[2,128,1024]{2,1,0:T(8,128)} %copy-done.19) | copy-start | bytes 3145732
  420.2 4.3 collective-permute-start.41
  420.5 16.1 %collective-permute-start.22 = (bf16[2,2,128,1024]{3,2,1,0:T(8,128)(2,1)S(1)}, bf16[2,2,128,1024]{3,2,1,0:T(8,128)(2,1)}, u32[]{:S(2)}, u32[]{:S(2)}) collective-permute-start(bf16[2,2,128,1024]{3,2,1,0:T(8,128)(2,1)S(1)} %fusion.18), channel_id=1, source_target_pairs={{0,1},{1,0},{2,3},{3,2},{4,5},{5,4},{6,7},{7,6},{8,9},{9,8},{10,11... | collective-permute-start | bytes 3145736 | tf_op jit(solution)/shard_map/ppermute | solution.py:21
  424.6 5.4 %collective-permute-start.42 = (f32[13,1024]{1,0:T(8,128)S(1)}, f32[13,1024]{1,0:T(8,128)S(1)}, u32[]{:S(2)}, u32[]{:S(2)}) collective-permute-start(f32[13,1024]{1,0:T(8,128)S(1)} %add.447), channel_id=1, source_target_pairs={{0,16},{4,20},{8,24},{12,28},{16,0},{20,4},{24,8},{28,12},{1,17},{... | collective-permute-start | bytes 159752 | tf_op jit(solution)/shard_map/ppermute | solution.py:21
  432.5 11.5 %collective-permute-start.28 = (bf16[8,32,1024]{2,1,0:T(8,128)(2,1)S(1)}, bf16[8,32,1024]{2,1,0:T(8,128)(2,1)S(1)}, u32[]{:S(2)}, u32[]{:S(2)}) collective-permute-start(bf16[8,32,1024]{2,1,0:T(8,128)(2,1)S(1)} %fusion.37), channel_id=1, source_target_pairs={{0,2},{1,3},{2,0},{3,1},{4,6},{5,7},{6,4},{7,5},{8,10},{9,11},{10,... | collective-permute-start | bytes 1572872 | tf_op jit(solution)/shard_map/ppermute | solution.py:21
  435.8 8.3 %collective-permute-start.25 = (bf16[2,128,768]{2,1,0:T(8,128)(2,1)S(1)}, bf16[2,128,768]{2,1,0:T(8,128)(2,1)S(1)}, u32[]{:S(2)}, u32[]{:S(2)}) collective-permute-start(bf16[2,128,768]{2,1,0:T(8,128)(2,1)S(1)} %fusion.50), channel_id=1, source_target_pairs={{0,8},{4,12},{8,0},{12,4},{16,24},{20,28},{24,16},{28,20},{1,9},{5... | collective-permute-start | bytes 1179656 | tf_op jit(solution)/shard_map/ppermute | solution.py:21
  444.3 8.7 %collective-permute-start.26 = (bf16[128,768]{1,0:T(8,128)(2,1)S(1)}, bf16[128,768]{1,0:T(8,128)(2,1)S(1)}, u32[]{:S(2)}, u32[]{:S(2)}) collective-permute-start(bf16[128,768]{1,0:T(8,128)(2,1)S(1)} %fusion.57), channel_id=1, source_target_pairs={{0,16},{4,20},{8,24},{12,28},{16,0},{20,4},{24,8},{28,12},{1,17},{... | collective-permute-start | bytes 589832 | tf_op jit(solution)/shard_map/ppermute | solution.py:21
  446.5 10.6 %collective-permute-start.29 = (bf16[2,2,32,1024]{3,2,0,1:T(8,128)(2,1)}, bf16[2,2,32,1024]{3,2,0,1:T(8,128)(2,1)}, u32[]{:S(2)}, u32[]{:S(2)}) collective-permute-start(bf16[2,2,32,1024]{3,2,0,1:T(8,128)(2,1)} %fusion.54), channel_id=1, source_target_pairs={{0,4},{4,0},{8,12},{12,8},{16,20},{20,16},{24,28},{28,24},{1,5},{5... | collective-permute-start | bytes 786440 | tf_op jit(solution)/shard_map/ppermute | solution.py:21
  448.9 20.0 %collective-permute-start.23 = (bf16[2,128,1024]{2,1,0:T(8,128)(2,1)}, bf16[2,128,1024]{2,1,0:T(8,128)(2,1)}, u32[]{:S(2)}, u32[]{:S(2)}) collective-permute-start(bf16[2,128,1024]{2,1,0:T(8,128)(2,1)} %fusion.36), channel_id=1, source_target_pairs={{0,2},{1,3},{2,0},{3,1},{4,6},{5,7},{6,4},{7,5},{8,10},{9,11},{10,... | collective-permute-start | bytes 1572872 | tf_op jit(solution)/shard_map/ppermute | solution.py:21
  453.7 8.7 %all-to-all-start.4 = ((bf16[4,32,768]{2,1,0:T(8,128)(2,1)}), bf16[4,32,768]{2,1,0:T(8,128)(2,1)S(1)}, u32[]{:S(2)}, u32[]{:S(2)}) async-start(bf16[4,32,768]{2,1,0:T(8,128)(2,1)} %bitcast.96), calls=%async_computation.4 | async-start | bytes 393216 | tf_op jit(solution)/shard_map/all_to_all | solution.py:86
  459.8 6.2 %collective-permute-start.30 = (bf16[2,32,1024]{2,1,0:T(8,128)(2,1)}, bf16[2,32,1024]{2,1,0:T(8,128)(2,1)}, u32[]{:S(2)}, u32[]{:S(2)}) collective-permute-start(bf16[2,32,1024]{2,1,0:T(8,128)(2,1)} %fusion.58), channel_id=1, source_target_pairs={{0,8},{4,12},{8,0},{12,4},{16,24},{20,28},{24,16},{28,20},{1,9},{5... | collective-permute-start | bytes 393224 | tf_op jit(solution)/shard_map/ppermute | solution.py:21
  467.0 6.2 %collective-permute-start.31 = (bf16[32,1024]{1,0:T(8,128)(2,1)S(1)}, bf16[32,1024]{1,0:T(8,128)(2,1)S(1)}, u32[]{:S(2)}, u32[]{:S(2)}) collective-permute-start(bf16[32,1024]{1,0:T(8,128)(2,1)S(1)} %fusion.59), channel_id=1, source_target_pairs={{0,16},{4,20},{8,24},{12,28},{16,0},{20,4},{24,8},{28,12},{1,17},{... | collective-permute-start | bytes 196616 | tf_op jit(solution)/shard_map/ppermute | solution.py:21
  (50 other events, 203.6 us)
Sparse Core Ops, SparseCore 0:
  11.5 74.5 all-gather.2
